TPU v7x, 256 devices: a whole 4x4x8 slice. The times are simulated.
256 devices in a mesh: row: 16 (over y_hi, x, core), tensor: 16 (over y_lo, z).
Axes of the slice: x: 4, y: 4 (y_hi: 2, y_lo: 2; y = y_hi * 2 + y_lo), z: 8, core: 2. Of those that a mesh axis runs over, the one named last changes fastest.
Arguments:
- latents: bfloat16 [4, 32, 64, 2240], P(None, 'row', None, 'tensor'), may hold values from -6 to 6
- clip_height: int32 [4], replicated, may hold values from 16 to 32, as said below
- clip_width: int32 [4], replicated, may hold values from 32 to 64, as said below
- expand_weight: bfloat16 [2, 2240, 5600], P(None, None, 'tensor'), may hold values from -0.125 to 0.125
- expand_bias: float32 [2, 5600], P(None, 'tensor'), may hold values from -3 to 3
- depth_weight: float32 [3, 3, 2, 5600], P(None, None, None, 'tensor'), may hold values from -2 to 2
- depth_bias: float32 [2, 5600], P(None, 'tensor'), may hold values from -3 to 3
- project_weight: bfloat16 [5600, 2240], P('tensor'), may hold values from -0.109375 to 0.109375
Outputs:
- block_output: bfloat16 [4, 32, 64, 2240], P(None, 'row', None, 'tensor')
Inputs may be any that keep to these rules, and one draw needn't show every extreme that they name: `clip_height`: one clip spans all 32 rows and another exactly 16 of them. `clip_width`: one clip spans all 64 columns and another exactly 32 of them.
All inputs are finite; a program needn't handle non-finite values.
Results may differ from a plain program's by a relative error of at most 0.0062.
Values may be sent and summed in bfloat16 or wider, within the bound.
A program may use at most 128 MiB of HBM per device.

v0:
```python
import jax
import jax.numpy as jnp
from jax import lax
from jax.sharding import PartitionSpec as P


def padded_2(cells, sides, width):
    for axis, dim in sides:
        count = lax.axis_size(axis)
        ends = count - 1
        head = lax.slice_in_dim(cells, 0, width, axis=dim)
        tail = lax.slice_in_dim(cells, cells.shape[dim] - width, cells.shape[dim], axis=dim)
        cells = jnp.concatenate(
            [
                lax.ppermute(tail, axis, [(i, (i + 1) % count) for i in range(ends)]),
                cells,
                lax.ppermute(head, axis, [((i + 1) % count, i) for i in range(ends)]),
            ],
            axis=dim,
        )
    return cells


def activate(pre_act, expand_bias, mask_rows):
    return (jax.nn.silu(pre_act + expand_bias) * mask_rows[..., None]).astype(jnp.bfloat16)


def depthwise(padded, depth_weight, depth_bias, row_count, col_count):
    widened = jnp.pad(padded, ((0, 0), (0, 0), (1, 1), (0, 0), (0, 0)))
    out_shape = (widened.shape[0], row_count, col_count) + widened.shape[3:]
    depth_out = jnp.zeros(out_shape, jnp.float32) + depth_bias
    for tap_row in range(3):
        for tap_col in range(3):
            depth_out = (
                depth_out
                + depth_weight[tap_row, tap_col]
                * widened[:, tap_row : tap_row + row_count, tap_col : tap_col + col_count]
            )
    return depth_out


def on_device(
    latents,
    clip_height,
    clip_width,
    expand_weight,
    expand_bias,
    depth_weight,
    depth_bias,
    project_weight,
):
    batch_size, row_count, col_count, _ = latents.shape
    first_row = lax.axis_index("row") * row_count
    row_ids = first_row + jnp.arange(row_count, dtype=jnp.int32)
    col_ids = jnp.arange(col_count, dtype=jnp.int32)
    valid_mask = (
        (row_ids[None, :, None] < clip_height[:, None, None])
        & (col_ids[None, None, :] < clip_width[:, None, None])
    ).astype(jnp.float32)[..., None]
    pre_act = jnp.einsum(
        "brcd,kdf->brckf",
        lax.all_gather(latents, "tensor", axis=3, tiled=True),
        expand_weight,
        preferred_element_type=jnp.float32,
    )
    expanded = activate(pre_act, expand_bias, valid_mask)
    padded = padded_2(expanded, (("row", 1),), 1)
    depth_out = depthwise(padded, depth_weight, depth_bias, row_count, col_count)
    hidden = (depth_out[:, :, :, 0] * jax.nn.silu(depth_out[:, :, :, 1])).astype(jnp.bfloat16)
    partial_term = jnp.einsum(
        "brcf,fd->brcd", hidden, project_weight, preferred_element_type=jnp.float32
    )
    summed = lax.psum_scatter(partial_term, "tensor", scatter_dimension=3, tiled=True)
    return (summed * valid_mask).astype(jnp.bfloat16)


def solution(mesh):
    in_specs = (
        P(None, "row", None, "tensor"),
        P(),
        P(),
        P(None, None, "tensor"),
        P(None, "tensor"),
        P(None, None, None, "tensor"),
        P(None, "tensor"),
        P("tensor", None),
    )
    out_specs = P(None, "row", None, "tensor")
    return jax.shard_map(
        on_device, mesh=mesh, in_specs=in_specs, out_specs=out_specs, check_vma=False
    )
```

profile of v0, /device:TPU:16, one launch (start us, length us, event | category | flops | bytes accessed | tf_op | source)
XLA Modules:
  0.0 278.7 jit_solution(2828875387564601945)
XLA Ops:
  6.5 0.0 copy-start
  6.5 0.0 all-gather.2.cloned.1.call-start
  6.5 2.1 copy.11
  8.6 0.0 all-gather.2.cloned.1.call-update
  8.6 0.0 all-reduce.4.cloned.1.call-start
  8.7 0.7 iota_compare_fusion.2
  9.4 0.7 broadcast_compare_fusion
  10.1 0.1 and_convert_fusion
  10.2 78.3 %all-gather.2.cloned.1.call-done = bf16[4,2,64,2240]{2,0,1,3:T(4,128)(2,1)} async-done(((bf16[4,2,64,140]{2,0,1,3:T(4,128)(2,1)}), bf16[4,2,64,2240]{2,0,1,3:T(4,128)(2,1)}) %all-gather.2.cloned.1.call-update) | async-done | bytes 2293776 | tf_op jit(solution)/shard_map/all_gather | solution.py:62
  88.5 0.0 copy-done
  88.5 6.2 %multiply_convert_fusion = bf16[4,2,64,2,350]{4,2,3,1,0:T(8,128)(2,1)S(1)} fusion(bf16[2,2240,350,1,1]{1,0,2,4,3:T(2,128)(2,1)S(1)} %bitcast.42, bf16[4,2,64,2240,1]{2,0,1,3,4:T(4,128)(2,1)} %bitcast.43, f32[4,2,64]{2,1,0:T(2,128)S(1)} %and_convert_fusion, f32[2,350]{1,0:T(2,128)} %param.12), kind=kOutput, calls=%fused_computation.14 | convolution fusion | flops 1608140800 | bytes 6151408 | tf_op jit(solution)/shard_map/brcd,kdf->brckf/dot_general | solution.py:60
  94.8 0.0 copy-start.2
  94.8 0.1 fusion.21
  94.9 1.9 collective-permute-start
  96.8 7.3 %collective-permute-start.1 = (bf16[4,1,64,2,350]{4,2,3,1,0:T(8,128)(2,1)S(1)}, bf16[4,1,64,2,350]{4,2,3,1,0:T(8,128)(2,1)S(1)}, u32[]{:S(2)}, u32[]{:S(2)}) collective-permute-start(bf16[4,1,64,2,350]{4,2,3,1,0:T(8,128)(2,1)S(1)} %get-tuple-element.6), channel_id=1, source_target_pairs={{16,0},{32,16},{48,32},{64,48},{80,64},{96,80},{112,96},{128,112},... | collective-permute-start | bytes 1075208 | tf_op jit(solution)/shard_map/ppermute | solution.py:17
  104.1 0.0 copy-done.2
  104.1 0.0 copy-start.3
  104.1 3.5 %collective-permute-done = bf16[4,1,64,2,350]{4,2,3,1,0:T(8,128)(2,1)S(1)} collective-permute-done((bf16[4,1,64,2,350]{4,2,3,1,0:T(8,128)(2,1)S(1)}, bf16[4,1,64,2,350]{4,2,3,1,0:T(8,128)(2,1)S(1)}, u32[]{:S(2)}, u32[]{:S(2)}) %collective-permute-start) | collective-permute-done | bytes 358432 | tf_op jit(solution)/shard_map/ppermute | solution.py:15
  107.6 1.8 collective-permute-done.1
  109.3 0.9 fusion.8
  110.2 0.0 copy-done.3
  110.2 0.0 copy-start.1
  110.2 1.7 multiply_add_fusion
  111.9 0.0 copy-done.1
  111.9 3.7 %fusion.9 = f32[4,2,64,2240]{3,2,1,0:T(8,128)} fusion(bf16[350,2240]{1,0:T(8,128)(2,1)S(1)} %copy-done.1, f32[4,2,64,2,350]{4,2,3,1,0:T(8,128)S(1)} %multiply_add_fusion), kind=kOutput, calls=%fused_computation.11 | convolution fusion | flops 803891200 | bytes 7589120 | tf_op jit(solution)/shard_map/brcf,fd->brcd/dot_general | solution.py:70
  115.6 0.0 copy-start.4
  115.6 0.0 all-reduce.4.cloned.1.call-update
  115.6 0.6 copy-done.4
  116.3 0.6 dynamic-slice
  117.5 152.3 %all-reduce.4.cloned.1.call-done = f32[4,2,64,2240]{3,2,1,0:T(8,128)} async-done(((f32[4,2,64,2240]{3,2,1,0:T(8,128)}), f32[4,2,64,2240]{3,2,1,0:T(8,128)}) %all-reduce.4.cloned.1.call-update) | async-done | bytes 4587536
  269.8 2.1 fusion.17
  (2 shorter events, 0.0 us)
Async XLA Ops:
  6.5 82.0 %copy-start = (bf16[2,2240,350]{1,0,2:T(2,128)(2,1)S(1)}, bf16[2,2240,350]{1,0,2:T(2,128)(2,1)}, u32[]{:S(2)}) copy-start(bf16[2,2240,350]{1,0,2:T(2,128)(2,1)} %param.11) | copy-start | bytes 9408004
  6.5 82.0 %all-gather.2.cloned.1.call-start = ((), (), s32[]{:S(2)}) async-start(), calls=%async_computation | async-start | bytes 4874240 | tf_op jit(solution)/shard_map/all_gather | solution.py:62
  8.6 261.2 %all-reduce.4.cloned.1.call-start = ((), (), s32[]{:S(2)}) async-start(), calls=%async_computation.1 | async-start | bytes 9437184
  94.8 9.3 %copy-start.2 = (f32[3,3,2,350]{3,2,1,0:T(2,128)S(1)}, f32[3,3,2,350]{3,2,1,0:T(2,128)}, u32[]{:S(2)}) copy-start(f32[3,3,2,350]{3,2,1,0:T(2,128)} %param.13) | copy-start | bytes 75604
  94.9 12.7 %collective-permute-start = (bf16[4,1,64,2,350]{4,2,3,1,0:T(8,128)(2,1)S(1)}, bf16[4,1,64,2,350]{4,2,3,1,0:T(8,128)(2,1)S(1)}, u32[]{:S(2)}, u32[]{:S(2)}) collective-permute-start(bf16[4,1,64,2,350]{4,2,3,1,0:T(8,128)(2,1)S(1)} %get-tuple-element.5), channel_id=1, source_target_pairs={{0,16},{16,32},{32,48},{48,64},{64,80},{80,96},{96,112},{112,128},... | collective-permute-start | bytes 1075208 | tf_op jit(solution)/shard_map/ppermute | solution.py:15
  96.8 12.5 %collective-permute-start.1 = (bf16[4,1,64,2,350]{4,2,3,1,0:T(8,128)(2,1)S(1)}, bf16[4,1,64,2,350]{4,2,3,1,0:T(8,128)(2,1)S(1)}, u32[]{:S(2)}, u32[]{:S(2)}) collective-permute-start(bf16[4,1,64,2,350]{4,2,3,1,0:T(8,128)(2,1)S(1)} %get-tuple-element.6), channel_id=1, source_target_pairs={{16,0},{32,16},{48,32},{64,48},{80,64},{96,80},{112,96},{128,112},... | collective-permute-start | bytes 1075208 | tf_op jit(solution)/shard_map/ppermute | solution.py:17
  104.1 6.1 %copy-start.3 = (f32[2,350]{1,0:T(2,128)S(1)}, f32[2,350]{1,0:T(2,128)}, u32[]{:S(2)}) copy-start(f32[2,350]{1,0:T(2,128)} %param.14) | copy-start | bytes 8404
  110.2 1.7 copy-start.1
  115.6 0.7 copy-start.4
Sparse Core Ops, SparseCore 0:
  9.1 79.3 all-gather.1
  115.7 154.0 all-reduce.3
where the time goes:
time: 280 us; the launch traced here: 279 us
  waiting for transfers between devices  236 us (84%)
  between operations  14.2 us (5%)
  matrix products  9.88 us (4%)
  starting transfers between devices  9.22 us (3%)
  other arithmetic  6.2 us (2%)
  local copies, waits for them, and re-layouts  3.41 us (1%)
    unnamed x3, waiting for transfers between devices  152 us
    all_gather x1, waiting for transfers between devices, on_device(): lax.all_gather(latents, 'tensor', axis=3, tiled=True)  78.3 us
    ppermute x1, starting transfers between devices, padded_2(): lax.ppermute(head, axis, [((i + 1) % count, i) for i in range(ends)])  7.26 us
    dot_general x1, matrix products, on_device(): jnp.einsum('brcd,kdf->brckf', lax.all_gather(latents, 'tensor', axis=3, t...  6.23 us
  transfers between devices with their start and end apart: 4, of which 4 were waited for; matrix products, arithmetic and copies ran while one was open for 1% of the time, Pallas kernels for 0%

commit v1 on v0

v1 whole, which is shorter than its diff:
```python
import functools

import jax
import jax.numpy as jnp
from jax import lax
from jax.experimental import pallas as pl
from jax.experimental.pallas import tpu as pltpu
from jax.sharding import PartitionSpec as P

MESH = pl.DeviceIdType.MESH
NY, NZ = 2, 8
LANES = 128
BF16 = jnp.bfloat16
F32 = jnp.float32


def ceil_to(n, m):
    return -(-n // m) * m


def silu(v):
    return v / (1.0 + jnp.exp(-v))


def kernel(
    rows,
    ch,
    x_ref,
    height_ref,
    width_ref,
    w_ref,
    cols_ref,
    p_ref,
    out_ref,
    xg,
    ex,
    dn_out,
    up_out,
    dn_in,
    up_in,
    hid,
    zc_out,
    zc_in,
    zw_out,
    zw_in,
    qc_out,
    qc_in,
    qw_out,
    qw_in,
    qy_out,
    qy_in,
    py_out,
    py_in,
    send,
    recv,
):
    r = lax.axis_index("row")
    t = lax.axis_index("tensor")
    y, z = t // NZ, t % NZ
    chp = xg.shape[3]
    ffp = ex.shape[2]
    width = xg.shape[4]
    per_half = width // LANES

    def tz(step):
        return (z + NZ + step) % NZ

    cw = {"tensor": y * NZ + tz(1)}
    ccw = {"tensor": y * NZ + tz(-1)}
    other = {"tensor": (1 - y) * NZ + z}
    above = {"row": (r + rows - 1) % rows}
    below = {"row": (r + 1) % rows}

    barrier = pltpu.get_barrier_semaphore()
    for target in (cw, ccw, other, above, below):
        pl.semaphore_signal(barrier, inc=1, device_id=target, device_id_type=MESH)

    ids = {}

    def copy(key, src, dst, target):
        n = ids.setdefault(key, len(ids))
        return pltpu.make_async_remote_copy(
            src_ref=src,
            dst_ref=dst,
            send_sem=send.at[n],
            recv_sem=recv.at[n],
            device_id=target,
            device_id_type=MESH,
        )

    pending = []

    def start(key, src, dst, target):
        c = copy(key, src, dst, target)
        c.start()
        pending.append(c)
        return c

    def block(half, zz, yy):
        return xg.at[half, zz, yy]

    for half in range(2):
        for b in range(per_half):
            tok = x_ref[half * per_half + b].reshape(LANES, ch)
            xg[half, z, y, 0:ch, b * LANES : (b + 1) * LANES] = tok.T
        xg[half, z, y, ch:chp, :] = jnp.zeros((chp - ch, width), BF16)

    pl.semaphore_wait(barrier, 5)

    y0 = start("y0", block(0, z, y), block(0, z, y), other)
    yq = {0: start("yq0", block(1, z, y), block(1, z, y), other)}
    pc, pw, qc, qw = {}, {}, {}, {}
    pc[0] = [start("pc0a", block(0, z, y), block(0, z, y), cw)]
    pw[0] = [start("pw0a", block(0, z, y), block(0, z, y), ccw)]
    qc[0] = start("qc0", block(1, z, y), block(1, z, y), cw)
    qw[0] = start("qw0", block(1, z, y), block(1, z, y), ccw)
    y0.wait_recv()
    pc[0].append(start("pc0b", block(0, z, 1 - y), block(0, z, 1 - y), cw))
    pw[0].append(start("pw0b", block(0, z, 1 - y), block(0, z, 1 - y), ccw))
    far_c, far_w = NZ // 2, NZ - 1 - NZ // 2
    for s in range(1, far_c + 1):
        for c in pc[s - 1]:
            c.wait_recv()
        if s < far_c:
            zz = tz(-s)
            pc[s] = [start(f"pc{s}", xg.at[0, zz], xg.at[0, zz], cw)]
        if s <= far_w:
            for c in pw[s - 1]:
                c.wait_recv()
            if s < far_w:
                zz = tz(s)
                pw[s] = [start(f"pw{s}", xg.at[0, zz], xg.at[0, zz], ccw)]
        qc[s - 1].wait_recv()
        zz = tz(-s)
        if s < far_c:
            qc[s] = start(f"qc{s}", block(1, zz, y), block(1, zz, y), cw)
        yq[-s] = start(f"yqc{s}", block(1, zz, y), block(1, zz, y), other)
        if s <= far_w:
            qw[s - 1].wait_recv()
            zz = tz(s)
            if s < far_w:
                qw[s] = start(f"qw{s}", block(1, zz, y), block(1, zz, y), ccw)
            yq[s] = start(f"yqw{s}", block(1, zz, y), block(1, zz, y), other)

    lane = lax.broadcasted_iota(jnp.int32, (1, LANES), 1)
    first = lane < LANES // 2
    col = lane % (LANES // 2)
    left_ok = col > 0
    right_ok = col < LANES // 2 - 1

    def valid(clip):
        h = 2 * r + lane // (LANES // 2)
        return (h < height_ref[clip]) & (col < width_ref[clip])

    top_ok = r > 0
    bottom_ok = r < rows - 1
    halo = {}

    def expand(half):
        gathered = xg[half].reshape(NZ * NY * chp, width)
        mask = jnp.concatenate(
            [valid(half * per_half + b).astype(F32) for b in range(per_half)], axis=1
        )
        for k in range(2):
            acc = jnp.dot(w_ref[k], gathered, preferred_element_type=F32)
            acc = silu(acc + cols_ref[:, k : k + 1]) * mask
            ex[half, k] = acc.astype(BF16)

        for b in range(per_half):
            sl = slice(b * LANES, (b + 1) * LANES)
            e0, e1 = ex[half, 0, :, sl].astype(F32), ex[half, 1, :, sl].astype(F32)
            dn_out[half, :, sl] = jnp.where(first, pltpu.roll(e0, LANES // 2, 1), e1).astype(BF16)
            up_out[half, :, sl] = jnp.where(first, e0, pltpu.roll(e1, LANES // 2, 1)).astype(BF16)
        halo[half] = (
            start(f"dn{half}", dn_out.at[half], dn_in.at[half], below),
            start(f"up{half}", up_out.at[half], up_in.at[half], above),
        )

    def conv(half):
        for c in halo[half]:
            c.wait_recv()
        for b in range(per_half):
            sl = slice(b * LANES, (b + 1) * LANES)
            up = jnp.where(top_ok, dn_in[half, :, sl].astype(F32), 0.0)
            dn = jnp.where(bottom_ok, up_in[half, :, sl].astype(F32), 0.0)
            outs = []
            for k in range(2):
                mid = ex[half, k, :, sl].astype(F32)
                turned = pltpu.roll(mid, LANES // 2, 1)
                a = up if k == 0 else pltpu.roll(up, LANES // 2, 1)
                d = pltpu.roll(dn, LANES // 2, 1) if k == 0 else dn
                taps = [jnp.where(first, a, turned), mid, jnp.where(first, turned, d)]
                sums = []
                for j in range(3):
                    total = None
                    for i in range(3):
                        n = 4 + (i * 3 + j) * 2 + k
                        term = cols_ref[:, n : n + 1] * taps[i]
                        total = term if total is None else total + term
                    sums.append(total)
                res = sums[1] + cols_ref[:, 2 + k : 3 + k]
                res = res + jnp.where(left_ok, pltpu.roll(sums[0], 1, 1), 0.0)
                res = res + jnp.where(right_ok, pltpu.roll(sums[2], LANES - 1, 1), 0.0)
                outs.append(res)
            hid[half, :, sl] = (outs[0] * silu(outs[1])).astype(BF16)

    def share(half, zz, yy=None):
        if yy is None:
            w = p_ref[zz].reshape(NY * chp, ffp)
        else:
            w = p_ref[zz, yy]
        return jnp.dot(w, hid[half], preferred_element_type=F32)

    pc[far_c - 1][0]
    expand(0)
    for c in yq.values():
        c.wait_recv()
    expand(1)
    conv(0)

    rc, rw, sc, sw = {}, {}, {}, {}

    def p_step(s):
        if s < far_c:
            total = share(0, tz(far_c - s))
            if s > 0:
                rc[s - 1].wait_recv()
                total = total + zc_in[s - 1].astype(F32)
            zc_out[s] = total.astype(BF16)
            rc[s] = start(f"rc{s}", zc_out.at[s], zc_in.at[s], cw)
        if s < far_w:
            total = share(0, tz(s - far_w))
            if s > 0:
                rw[s - 1].wait_recv()
                total = total + zw_in[s - 1].astype(F32)
            zw_out[s] = total.astype(BF16)
            rw[s] = start(f"rw{s}", zw_out.at[s], zw_in.at[s], ccw)

    p_step(0)
    conv(1)
    order = []
    for s in range(far_c):
        order.append(far_c - s)
        if s < far_w:
            order.append(s - far_w)
    order.append(0)
    qy = {}
    for n, d in enumerate(order):
        qy_out[n] = share(1, tz(d), 1 - y).astype(BF16)
        qy[d] = (n, start(f"qy{n}", qy_out.at[n], qy_in.at[n], other))

    def q_block(d):
        n, c = qy[d]
        total = share(1, tz(d), y)
        c.wait_recv()
        return total + qy_in[n].astype(F32)

    def q_step(s):
        if s < far_c:
            total = q_block(far_c - s)
            if s > 0:
                sc[s - 1].wait_recv()
                total = total + qc_in[s - 1].astype(F32)
            qc_out[s] = total.astype(BF16)
            sc[s] = start(f"sc{s}", qc_out.at[s], qc_in.at[s], cw)
        if s < far_w:
            total = q_block(s - far_w)
            if s > 0:
                sw[s - 1].wait_recv()
                total = total + qw_in[s - 1].astype(F32)
            qw_out[s] = total.astype(BF16)
            sw[s] = start(f"sw{s}", qw_out.at[s], qw_in.at[s], ccw)

    for s in range(far_c):
        q_step(s)
        p_step(s + 1)

    def emit(half, total):
        for b in range(per_half):
            clip = half * per_half + b
            part = total[:, b * LANES : (b + 1) * LANES]
            part = jnp.where(valid(clip), part, 0.0)
            tok = part.T[:, :ch].astype(BF16)
            out_ref[clip] = tok.reshape(out_ref.shape[1:])

    rc[far_c - 1].wait_recv()
    rw[far_w - 1].wait_recv()
    whole = share(0, z, 1 - y)
    py_out[...] = (
        whole
        + zc_in[far_c - 1, pl.ds((1 - y) * chp, chp)].astype(F32)
        + zw_in[far_w - 1, pl.ds((1 - y) * chp, chp)].astype(F32)
    ).astype(BF16)
    last = start("py", py_out, py_in, other)
    mine = (
        share(0, z, y)
        + zc_in[far_c - 1, pl.ds(y * chp, chp)].astype(F32)
        + zw_in[far_w - 1, pl.ds(y * chp, chp)].astype(F32)
    )
    total = q_block(0)
    sc[far_c - 1].wait_recv()
    sw[far_w - 1].wait_recv()
    total = total + qc_in[far_c - 1].astype(F32) + qw_in[far_w - 1].astype(F32)
    emit(1, total)
    last.wait_recv()
    emit(0, mine + py_in[...].astype(F32))
    for c in pending:
        c.wait_send()


def on_device(
    row_devices,
    latents,
    clip_height,
    clip_width,
    expand_weight,
    expand_bias,
    depth_weight,
    depth_bias,
    project_weight,
):
    batch, row_count, col_count, ch = latents.shape
    ff = expand_bias.shape[1]
    assert row_count * col_count == LANES and batch % 2 == 0
    chp, ffp = ceil_to(ch, 16), ceil_to(ff, 16)
    width = batch // 2 * LANES

    w = expand_weight.transpose(0, 2, 1).reshape(2, ff, NY, NZ, ch).transpose(0, 1, 3, 2, 4)
    w = jnp.pad(w, ((0, 0), (0, ffp - ff), (0, 0), (0, 0), (0, chp - ch)))
    w = w.reshape(2, ffp, NZ * NY * chp)
    p = project_weight.reshape(ff, NY, NZ, ch).transpose(2, 1, 3, 0)
    p = jnp.pad(p, ((0, 0), (0, 0), (0, chp - ch), (0, ffp - ff)))
    cols = jnp.concatenate([expand_bias, depth_bias, depth_weight.reshape(18, ff)], axis=0)
    cols = jnp.pad(cols.T, ((0, ffp - ff), (0, 0)))

    far_c, far_w = NZ // 2, NZ - 1 - NZ // 2
    vmem = pl.BlockSpec(memory_space=pltpu.VMEM)
    smem = pl.BlockSpec(memory_space=pltpu.SMEM)
    return pl.pallas_call(
        functools.partial(kernel, row_devices, ch),
        out_shape=jax.ShapeDtypeStruct(latents.shape, BF16),
        in_specs=[vmem, smem, smem, vmem, vmem, vmem],
        out_specs=vmem,
        scratch_shapes=[
            pltpu.VMEM((2, NZ, NY, chp, width), BF16),
            pltpu.VMEM((2, 2, ffp, width), BF16),
        ]
        + [pltpu.VMEM((2, ffp, width), BF16)] * 5
        + [pltpu.VMEM((far_c, NY * chp, width), BF16)] * 2
        + [pltpu.VMEM((far_w, NY * chp, width), BF16)] * 2
        + [pltpu.VMEM((far_c, chp, width), BF16)] * 2
        + [pltpu.VMEM((far_w, chp, width), BF16)] * 2
        + [pltpu.VMEM((NZ, chp, width), BF16)] * 2
        + [pltpu.VMEM((chp, width), BF16)] * 2
        + [pltpu.SemaphoreType.DMA((64,)), pltpu.SemaphoreType.DMA((64,))],
        compiler_params=pltpu.CompilerParams(
            collective_id=0, has_side_effects=True, vmem_limit_bytes=60 * 1024 * 1024
        ),
    )(latents, clip_height, clip_width, w, cols, p)


def solution(mesh):
    in_specs = (
        P(None, "row", None, "tensor"),
        P(),
        P(),
        P(None, None, "tensor"),
        P(None, "tensor"),
        P(None, None, None, "tensor"),
        P(None, "tensor"),
        P("tensor", None),
    )
    return jax.shard_map(
        functools.partial(on_device, mesh.shape["row"]),
        mesh=mesh,
        in_specs=in_specs,
        out_specs=P(None, "row", None, "tensor"),
        check_vma=False,
    )
```

time: 280 us -> 113 us (0.40)
  the two profiles are of different devices: /device:TPU:16 before, /device:TPU:32 now
where the time goes in v1:
time: 113 us
  Pallas kernels  75.4 us (67%)
  local copies, waits for them, and re-layouts  37.2 us (33%)
    pallas_call x1, Pallas kernels, on_device(): pl.pallas_call(functools.partial(kernel, row_devices, ch), out_shape=jax....  75.4 us
    reshape x2, local copies, waits for them, and re-layouts, on_device(): p = project_weight.reshape(ff, NY, NZ, ch).transpose(2, 1, 3, 0)  12.3 us
    transpose x1, local copies, waits for them, and re-layouts, on_device(): expand_weight.transpose(0, 2, 1).reshape(2, ff, NY, NZ, ch)  10.4 us
    reshape x1, local copies, waits for them, and re-layouts, on_device(): expand_weight.transpose(0, 2, 1).reshape(2, ff, NY, NZ, ch)  4.29 us
    reshape x1, local copies, waits for them, and re-layouts, on_device(): w = w.reshape(2, ffp, NZ * NY * chp)  4.01 us
    pad x1, local copies, waits for them, and re-layouts, on_device(): p = jnp.pad(p, ((0, 0), (0, 0), (0, chp - ch), (0, ffp - ff)))  2.89 us

profile of v1, /device:TPU:32, one launch (start us, length us, event | category | flops | bytes accessed | tf_op | source)
XLA Modules:
  0.0 112.7 jit_solution(11509529958488959290)
XLA Ops:
  0.0 10.4 %copy.21 = bf16[2,350,2240]{1,2,0:T(8,128)(2,1)} copy(bf16[2,350,2240]{2,0,1:T(2,128)(2,1)} %bitcast.10) | data formatting | bytes 6272000 | tf_op jit(solution)/shard_map/transpose | solution.py:328
  10.4 4.3 %reshape.12 = bf16[2,350,2,8,140]{1,4,3,2,0:T(8,128)(2,1)S(1)} reshape(bf16[2,350,2240]{1,2,0:T(8,128)(2,1)} %copy.21) | data formatting | bytes 6272000 | tf_op jit(solution)/shard_map/reshape | solution.py:328
  14.7 0.4 copy.29
  15.1 0.4 pad.12.clone
  15.5 4.0 %copy.26.w_ref = bf16[2,352,2304]{2,1,0:T(8,128)(2,1)} copy(bf16[2,352,2304]{1,2,0:T(8,128)(2,1)S(1)} %bitcast.7) | data formatting | bytes 6488064 | tf_op jit(solution)/shard_map/reshape | solution.py:330
  19.5 9.1 %reshape.16 = bf16[350,2,8,140]{3,2,1,0:T(8,128)(2,1)S(1)} reshape(bf16[350,2240]{1,0:T(8,128)(2,1)} %param.15) | data formatting | bytes 3136000 | tf_op jit(solution)/shard_map/reshape | solution.py:331
  28.6 0.0 copy-start
  28.6 0.0 copy-start.1
  28.7 0.0 copy-start.2
  28.7 3.2 %copy.25 = bf16[350,2,8,140]{0,3,1,2:T(8,128)(2,1)} copy(bf16[350,2,8,140]{3,2,1,0:T(8,128)(2,1)S(1)} %reshape.16) | data formatting | bytes 3136000 | tf_op jit(solution)/shard_map/reshape | solution.py:331
  31.8 2.9 %pad.14.p_ref = bf16[8,2,144,352]{3,2,1,0:T(8,128)(2,1)} pad(bf16[8,2,140,350]{3,2,1,0:T(8,128)(2,1)} %bitcast.9, bf16[]{:T(256)} %constant.3.clone.1), padding=0_0x0_0x0_4x0_2 | pad | bytes 3190018 | tf_op jit(solution)/shard_map/jit(_pad)/pad | solution.py:332
  34.7 0.0 copy-done
  34.8 0.0 copy-done.1
  34.8 0.0 copy-done.2
  34.8 0.1 copy.23
  34.9 0.7 pad.13.cols_ref
  35.6 75.4 %shard_map.82 = bf16[4,2,64,140]{3,2,1,0:T(8,128)(2,1)} custom-call(bf16[4,2,64,140]{3,2,1,0:T(8,128)(2,1)} %x_ref.1, s32[4]{0:T(128)} %height_ref.1, s32[4]{0:T(128)} %width_ref.1, bf16[2,352,2304]{2,1,0:T(8,128)(2,1)} %copy.26.w_ref, f32[352,22]{1,0:T(8,128)} %pad.13.cols_ref, bf16[8,2,144,352]{3,2,1,0:T(8,128)(2,1)} %pad.14.p_ref), custom_call_target="tpu_custom_call" | custom-call | tf_op jit(solution)/shard_map/pallas_call | solution.py:339
  111.0 1.7 %copy.31 = bf16[4,2,64,140]{3,2,1,0:T(8,128)(2,1)} copy(bf16[4,2,64,140]{3,2,1,0:T(8,128)(2,1)} %shard_map.82) | data formatting | bytes 286720
  (2 shorter events, 0.0 us)
Async XLA Ops:
  28.6 6.1 %copy-start = (f32[3,3,2,350]{3,2,1,0:T(2,128)S(1)}, f32[3,3,2,350]{3,2,1,0:T(2,128)}, u32[]{:S(2)}) copy-start(f32[3,3,2,350]{3,2,1,0:T(2,128)} %param.13) | copy-start | bytes 75604
  28.6 6.1 %copy-start.1 = (f32[2,350]{1,0:T(2,128)S(1)}, f32[2,350]{1,0:T(2,128)}, u32[]{:S(2)}) copy-start(f32[2,350]{1,0:T(2,128)} %param.14) | copy-start | bytes 8404
  28.7 6.1 %copy-start.2 = (f32[2,350]{1,0:T(2,128)S(1)}, f32[2,350]{1,0:T(2,128)}, u32[]{:S(2)}) copy-start(f32[2,350]{1,0:T(2,128)} %param.12) | copy-start | bytes 8404

commit v2 on v1

--- a/solution.py
+++ b/solution.py
@@ -28,10 +28,19 @@
     x_ref,
     height_ref,
     width_ref,
+    w_hbm,
+    bias_ref,
+    taps_ref,
+    shift_ref,
+    p_hbm,
+    out_ref,
+    w_raw,
+    w_flat,
     w_ref,
+    p_raw,
+    p_ref,
+    rows_s,
     cols_ref,
-    p_ref,
-    out_ref,
     xg,
     ex,
     dn_out,
@@ -51,15 +60,18 @@
     qy_in,
     py_out,
     py_in,
+    load,
     send,
     recv,
 ):
     r = lax.axis_index("row")
     t = lax.axis_index("tensor")
     y, z = t // NZ, t % NZ
+    ff = bias_ref.shape[1]
     chp = xg.shape[3]
     ffp = ex.shape[2]
     width = xg.shape[4]
+    wide = NY * NZ * ch
     per_half = width // LANES
 
     def tz(step):
@@ -70,6 +82,11 @@
     other = {"tensor": (1 - y) * NZ + z}
     above = {"row": (r + rows - 1) % rows}
     below = {"row": (r + 1) % rows}
+
+    w_load = pltpu.make_async_copy(w_hbm, w_raw.at[pl.ds(0, ff)], load.at[0])
+    p_load = pltpu.make_async_copy(p_hbm, p_raw, load.at[1])
+    w_load.start()
+    p_load.start()
 
     barrier = pltpu.get_barrier_semaphore()
     for target in (cw, ccw, other, above, below):
@@ -97,15 +114,72 @@
         return c
 
     def block(half, zz, yy):
-        return xg.at[half, zz, yy]
+        return xg.at[half, yy, zz]
 
     for half in range(2):
         for b in range(per_half):
             tok = x_ref[half * per_half + b].reshape(LANES, ch)
-            xg[half, z, y, 0:ch, b * LANES : (b + 1) * LANES] = tok.T
-        xg[half, z, y, ch:chp, :] = jnp.zeros((chp - ch, width), BF16)
+            xg[half, y, z, 0:ch, b * LANES : (b + 1) * LANES] = tok.T
+        xg[half, y, z, ch:chp, :] = jnp.zeros((chp - ch, width), BF16)
 
     pl.semaphore_wait(barrier, 5)
+
+    def flatten_w():
+        w_flat[:, wide:] = jnp.zeros((2 * ffp, w_flat.shape[1] - wide), BF16)
+        w_load.wait()
+        w_raw[ff:ffp] = jnp.zeros((ffp - ff, 2, wide), BF16)
+
+        def body(i, _):
+            dst = pl.ds(pl.multiple_of(i * 32, 32), 32)
+            w_flat[dst, 0:wide] = w_raw[pl.ds(i * 16, 16)].reshape(32, wide)
+            return 0
+
+        lax.fori_loop(0, ffp // 16, body, 0)
+
+    def spread_w():
+        for j in range(NY * NZ * chp // LANES):
+            c = LANES * j + lax.broadcasted_iota(jnp.int32, (2 * LANES, LANES), 1)
+            begin = LANES * j - (chp - ch) * (LANES * j // chp)
+            base = begin // LANES * LANES
+            p = base + lax.broadcasted_iota(jnp.int32, (2 * LANES, LANES), 0)
+            owner = c // chp
+            pick = (p == c - (chp - ch) * owner) & (c - chp * owner < ch)
+            part = jnp.dot(
+                w_flat[:, base : base + 2 * LANES],
+                pick.astype(F32).astype(BF16),
+                preferred_element_type=F32,
+            )
+            w_ref[:, LANES * j : LANES * (j + 1)] = part.astype(BF16)
+
+    def split_w():
+        to = lax.broadcasted_iota(jnp.int32, (2 * ffp, 2 * ffp), 0)
+        at = lax.broadcasted_iota(jnp.int32, (2 * ffp, 2 * ffp), 1)
+        pick = at == jnp.where(to < ffp, 2 * to, 2 * (to - ffp) + 1)
+        pick = pick.astype(F32).astype(BF16)
+        for n in range(NY * NZ * chp // (2 * LANES)):
+            sl = slice(2 * LANES * n, 2 * LANES * (n + 1))
+            part = jnp.dot(pick, w_ref[:, sl], preferred_element_type=F32)
+            w_ref[:, sl] = part.astype(BF16)
+
+    def turn_p():
+        p_ref[...] = jnp.zeros_like(p_ref)
+        p_load.wait()
+        for zz in range(NZ):
+            for yy in range(NY):
+                o = yy * NZ + zz
+                p_ref[zz, yy, 0:ch, 0:ff] = p_raw[:, ch * o : ch * (o + 1)].T
+
+    def turn_columns():
+        rows_s[...] = jnp.zeros_like(rows_s)
+        rows_s[0:2, 0:ff] = bias_ref[...]
+        rows_s[2:4, 0:ff] = shift_ref[...]
+        for i in range(3):
+            for j in range(3):
+                n = 4 + 2 * (3 * i + j)
+                rows_s[n : n + 2, 0:ff] = taps_ref[i, j]
+        cols_ref[...] = rows_s[...].T[:ffp]
+
+    work = {1: spread_w, 2: split_w, 3: turn_p}
 
     y0 = start("y0", block(0, z, y), block(0, z, y), other)
     yq = {0: start("yq0", block(1, z, y), block(1, z, y), other)}
@@ -114,6 +188,8 @@
     pw[0] = [start("pw0a", block(0, z, y), block(0, z, y), ccw)]
     qc[0] = start("qc0", block(1, z, y), block(1, z, y), cw)
     qw[0] = start("qw0", block(1, z, y), block(1, z, y), ccw)
+    turn_columns()
+    flatten_w()
     y0.wait_recv()
     pc[0].append(start("pc0b", block(0, z, 1 - y), block(0, z, 1 - y), cw))
     pw[0].append(start("pw0b", block(0, z, 1 - y), block(0, z, 1 - y), ccw))
@@ -123,13 +199,13 @@
             c.wait_recv()
         if s < far_c:
             zz = tz(-s)
-            pc[s] = [start(f"pc{s}", xg.at[0, zz], xg.at[0, zz], cw)]
+            pc[s] = [start(f"pc{s}", xg.at[0, :, zz], xg.at[0, :, zz], cw)]
         if s <= far_w:
             for c in pw[s - 1]:
                 c.wait_recv()
             if s < far_w:
                 zz = tz(s)
-                pw[s] = [start(f"pw{s}", xg.at[0, zz], xg.at[0, zz], ccw)]
+                pw[s] = [start(f"pw{s}", xg.at[0, :, zz], xg.at[0, :, zz], ccw)]
         qc[s - 1].wait_recv()
         zz = tz(-s)
         if s < far_c:
@@ -141,6 +217,8 @@
             if s < far_w:
                 qw[s] = start(f"qw{s}", block(1, zz, y), block(1, zz, y), ccw)
             yq[s] = start(f"yqw{s}", block(1, zz, y), block(1, zz, y), other)
+        if s in work:
+            work[s]()
 
     lane = lax.broadcasted_iota(jnp.int32, (1, LANES), 1)
     first = lane < LANES // 2
@@ -162,7 +240,7 @@
             [valid(half * per_half + b).astype(F32) for b in range(per_half)], axis=1
         )
         for k in range(2):
-            acc = jnp.dot(w_ref[k], gathered, preferred_element_type=F32)
+            acc = jnp.dot(w_ref[k * ffp : (k + 1) * ffp], gathered, preferred_element_type=F32)
             acc = silu(acc + cols_ref[:, k : k + 1]) * mask
             ex[half, k] = acc.astype(BF16)
 
@@ -325,24 +403,25 @@
     chp, ffp = ceil_to(ch, 16), ceil_to(ff, 16)
     width = batch // 2 * LANES
 
-    w = expand_weight.transpose(0, 2, 1).reshape(2, ff, NY, NZ, ch).transpose(0, 1, 3, 2, 4)
-    w = jnp.pad(w, ((0, 0), (0, ffp - ff), (0, 0), (0, 0), (0, chp - ch)))
-    w = w.reshape(2, ffp, NZ * NY * chp)
-    p = project_weight.reshape(ff, NY, NZ, ch).transpose(2, 1, 3, 0)
-    p = jnp.pad(p, ((0, 0), (0, 0), (0, chp - ch), (0, ffp - ff)))
-    cols = jnp.concatenate([expand_bias, depth_bias, depth_weight.reshape(18, ff)], axis=0)
-    cols = jnp.pad(cols.T, ((0, ffp - ff), (0, 0)))
-
     far_c, far_w = NZ // 2, NZ - 1 - NZ // 2
     vmem = pl.BlockSpec(memory_space=pltpu.VMEM)
+    hbm = pl.BlockSpec(memory_space=pl.ANY)
+    flat = ceil_to(NY * NZ * chp, LANES) + LANES
     smem = pl.BlockSpec(memory_space=pltpu.SMEM)
     return pl.pallas_call(
         functools.partial(kernel, row_devices, ch),
         out_shape=jax.ShapeDtypeStruct(latents.shape, BF16),
-        in_specs=[vmem, smem, smem, vmem, vmem, vmem],
+        in_specs=[vmem, smem, smem, hbm, vmem, vmem, vmem, hbm],
         out_specs=vmem,
         scratch_shapes=[
-            pltpu.VMEM((2, NZ, NY, chp, width), BF16),
+            pltpu.VMEM((ffp, 2, NY * NZ * ch), BF16),
+            pltpu.VMEM((2 * ffp, flat), BF16),
+            pltpu.VMEM((2 * ffp, NY * NZ * chp), BF16),
+            pltpu.VMEM((ff, NY * NZ * ch), BF16),
+            pltpu.VMEM((NZ, NY, chp, ffp), BF16),
+            pltpu.VMEM((LANES, ceil_to(ffp, LANES)), F32),
+            pltpu.VMEM((ffp, LANES), F32),
+            pltpu.VMEM((2, NY, NZ, chp, width), BF16),
             pltpu.VMEM((2, 2, ffp, width), BF16),
         ]
         + [pltpu.VMEM((2, ffp, width), BF16)] * 5
@@ -352,11 +431,20 @@
         + [pltpu.VMEM((far_w, chp, width), BF16)] * 2
         + [pltpu.VMEM((NZ, chp, width), BF16)] * 2
         + [pltpu.VMEM((chp, width), BF16)] * 2
-        + [pltpu.SemaphoreType.DMA((64,)), pltpu.SemaphoreType.DMA((64,))],
+        + [pltpu.SemaphoreType.DMA((2,)), pltpu.SemaphoreType.DMA((64,)), pltpu.SemaphoreType.DMA((64,))],
         compiler_params=pltpu.CompilerParams(
             collective_id=0, has_side_effects=True, vmem_limit_bytes=60 * 1024 * 1024
         ),
-    )(latents, clip_height, clip_width, w, cols, p)
+    )(
+        latents,
+        clip_height,
+        clip_width,
+        expand_weight.transpose(2, 0, 1),
+        expand_bias,
+        depth_weight,
+        depth_bias,
+        project_weight,
+    )
 
 
 def solution(mesh):

time: 113 us -> 75.8 us (0.67)
  local copies, waits for them, and re-layouts: 37.2 us -> 1.67 us
  Pallas kernels: 75.4 us -> 74 us
    reshape x5 -> x0, local copies, waits for them, and re-layouts: 20.6 us -> none  [the longest x2 12.3 us: on_device(): p = project_weight.reshape(ff, NY, NZ, ch).transpose(2, 1, 3, 0)]
    transpose x1 -> x0, local copies, waits for them, and re-layouts: 10.4 us -> none  [on_device(): expand_weight.transpose(0, 2, 1).reshape(2, ff, NY, NZ, ch)]
    pad x3 -> x0, local copies, waits for them, and re-layouts: 3.98 us -> none  [the longest x1 2.89 us: on_device(): p = jnp.pad(p, ((0, 0), (0, 0), (0, chp - ch), (0, ffp - ff)))]
    pallas_call x1, Pallas kernels: 75.4 us -> 74 us  [on_device(): pl.pallas_call(functools.partial(kernel, row_devices, ch), out_shape=jax....]
where the time goes in v2:
time: 75.8 us; the launch traced here: 75.7 us
  Pallas kernels  74 us (98%)
  local copies, waits for them, and re-layouts  1.67 us (2%)
    pallas_call x1, Pallas kernels, on_device(): pl.pallas_call(functools.partial(kernel, row_devices, ch), out_shape=jax....  74 us
    unnamed x1, local copies, waits for them, and re-layouts  1.67 us

profile of v2, /device:TPU:32, one launch (start us, length us, event | category | flops | bytes accessed | tf_op | source)
XLA Modules:
  0.0 75.7 jit_solution(15126180063358453682)
XLA Ops:
  0.0 74.0 %shard_map.82 = bf16[4,2,64,140]{3,2,1,0:T(8,128)(2,1)} custom-call(bf16[4,2,64,140]{3,2,1,0:T(8,128)(2,1)} %x_ref.1, s32[4]{0:T(128)} %height_ref.1, s32[4]{0:T(128)} %width_ref.1, bf16[350,2,2240]{2,1,0:T(2,128)(2,1)} %bitcast.1, f32[2,350]{1,0:T(2,128)} %bias_ref.1, f32[3,3,2,350]{3,2,1,0:T(2,128)} %taps_ref.1, f32[2,350]{1,0:T(2,128)} %shift_ref.1, ...), custom_call_target="tpu_custom_call" | custom-call | tf_op jit(solution)/shard_map/pallas_call | solution.py:411
  74.0 1.7 %copy.10 = bf16[4,2,64,140]{3,2,1,0:T(8,128)(2,1)} copy(bf16[4,2,64,140]{3,2,1,0:T(8,128)(2,1)} %shard_map.82) | data formatting | bytes 286720

commit v3 on v0

v3 whole, which is shorter than its diff:
```python
import functools

import jax
import jax.numpy as jnp
from jax import lax
from jax.experimental import pallas as pl
from jax.experimental.pallas import tpu as pltpu
from jax.sharding import PartitionSpec as P

MESH = pl.DeviceIdType.MESH
NY, NZ = 2, 8
FAR = NZ // 2
LANES = 128
HALF = LANES // 2
PAIR = 2 * LANES
BF16 = jnp.bfloat16
F32 = jnp.float32
NEAR_ORDER = (4, 3, -3, 2, -2, 1, -1, 0)


def ceil_to(n, m):
    return -(-n // m) * m


def silu(v):
    return v / (1.0 + jnp.exp(-v))


def iota(shape, dim):
    return lax.broadcasted_iota(jnp.int32, shape, dim)


def one_hot(cond):
    return jnp.where(cond, 1.0, 0.0).astype(BF16)


def across(a, b):
    return lax.dot_general(a, b, (((1,), (1,)), ((), ())), preferred_element_type=F32)


def kernel(
    rows,
    x_ref,
    height_ref,
    width_ref,
    w_hbm,
    bias_ref,
    taps_ref,
    shift_ref,
    p_hbm,
    out_ref,
    w_raw,
    w_flat,
    w_ref,
    p_raw,
    p_ref,
    rows_s,
    cols_s,
    taps_s,
    place,
    spot,
    xp_full,
    xp_half,
    xq,
    hx_out,
    hx_in,
    ec,
    ex,
    dn_out,
    up_out,
    dn_in,
    up_in,
    hid,
    hc,
    part,
    pf_out,
    pf_in,
    ph_out,
    ph_in,
    qz_out,
    qz_in,
    qy_out,
    qy_in,
    py_out,
    py_in,
    load,
    send,
    recv,
):
    r = lax.axis_index("row")
    t = lax.axis_index("tensor")
    y, z = t // NZ, t % NZ
    clips, row_count, col_count, ch = x_ref.shape
    ff, ffp, chp = bias_ref.shape[1], ex.shape[1], xq.shape[3]
    wide, spread = NY * NZ * ch, NY * NZ * chp
    cut = ceil_to(chp // 2, 16)

    def tz(step):
        return (z + NZ + step) % NZ

    ring = ({"tensor": y * NZ + tz(1)}, {"tensor": y * NZ + tz(-1)})
    other = {"tensor": (1 - y) * NZ + z}
    above = {"row": (r + rows - 1) % rows}
    below = {"row": (r + 1) % rows}

    w_load = pltpu.make_async_copy(w_hbm, w_raw.at[pl.ds(0, ff)], load.at[0])
    p_load = pltpu.make_async_copy(p_hbm, p_raw, load.at[1])
    w_load.start()
    p_load.start()

    barrier = pltpu.get_barrier_semaphore()
    for target in ring + (other, above, below):
        pl.semaphore_signal(barrier, inc=1, device_id=target, device_id_type=MESH)

    pending = {}

    def start(key, src, dst, target):
        n = len(pending)
        c = pltpu.make_async_remote_copy(
            src_ref=src,
            dst_ref=dst,
            send_sem=send.at[n],
            recv_sem=recv.at[n],
            device_id=target,
            device_id_type=MESH,
        )
        c.start()
        pending[key] = c

    def same(key, ref, target):
        start(key, ref, ref, target)

    def arrived(*key):
        pending[key].wait_recv()

    widths = [width_ref[b] for b in range(clips)]
    heights = [height_ref[b] for b in range(clips)]
    narrow = jnp.int32(clips - 1)
    for b in reversed(range(clips - 1)):
        narrow = jnp.where(widths[b] == col_count // 2, b, narrow)
    slots = [jnp.where(narrow == b, clips - 1, jnp.where(narrow < b, b - 1, b)) for b in range(clips)]

    def of_slot(s, values):
        total = jnp.int32(0)
        for b in range(clips):
            total = total + jnp.where(slots[b] == s, values[b], 0)
        return total

    slot_w = [of_slot(s, widths) for s in range(clips)]
    slot_h = [of_slot(s, heights) for s in range(clips)]

    sub, lane2 = iota((LANES, PAIR), 0), iota((LANES, PAIR), 1)
    sub_row, sub_col = sub // HALF, sub % HALF
    canvas_row = row_count * r + sub_row

    def make_place():
        for g in range(2):
            for b in range(clips):
                limit = jnp.where(slots[b] // 2 == g, widths[b], 0)
                first_slot = jnp.where(slots[b] == 2 * g + 1, 2 * slot_w[2 * g], 0)
                a = first_slot + sub_row * widths[b] + sub_col
                if g == 1:
                    a = jnp.where(a < HALF, a + HALF * y, a + HALF)
                ok = (sub_col < limit) & (canvas_row < heights[b])
                place[g, b * LANES : (b + 1) * LANES] = one_hot(ok & (lane2 == a))

    def make_spot():
        for g in range(2):
            for s in range(2):
                w, h = slot_w[2 * g + s], slot_h[2 * g + s]
                a = s * 2 * slot_w[2 * g] + sub_row * w + sub_col
                ok = (sub_col < w) & (canvas_row < h)
                if g == 0:
                    hit = lane2 == a
                else:
                    hit = (lane2 == a + HALF) | ((a < HALF) & (lane2 == a))
                spot[g, s * LANES : (s + 1) * LANES] = one_hot(ok & hit)

    make_place()
    tokens = x_ref[...].reshape(clips * LANES, ch).T
    for g in range(2):
        block = jnp.dot(tokens, place[g], preferred_element_type=F32).astype(BF16)
        empty = jnp.zeros((chp - ch, LANES), BF16)
        if g == 0:
            xp_full[y, z, 0:ch] = block[:, :LANES]
            xp_full[y, z, ch:chp] = empty
        else:
            hx_out[0:ch] = block[:, :LANES]
            hx_out[ch:chp] = empty
        xq[g, y, z, 0:ch] = block[:, LANES:]
        xq[g, y, z, ch:chp] = empty

    pl.semaphore_wait(barrier, 5)

    def gather_begin(g):
        if g == 0:
            same((g, "y"), xp_full.at[y, z], other)
            for d in range(2):
                same((g, "own", d), xp_full.at[y, z], ring[d])
        else:
            start((g, "y"), hx_out, hx_in, other)
        for d in range(2):
            same((g, "q", d, 0), xq.at[g, y, z], ring[d])
        same((g, "qy", 0), xq.at[g, y, z], other)

    def gather_pair(g):
        arrived(g, "y")
        if g == 0:
            for d in range(2):
                same((g, "p", d, 0), xp_full.at[1 - y, z], ring[d])
        else:
            xp_half[z] = hx_out[...] + hx_in[...]
            for d in range(2):
                same((g, "p", d, 0), xp_half.at[z], ring[d])

    def gather_step(g, s):
        for d in range(2):
            zz = tz(-s if d == 0 else s)
            arrived(g, "p", d, s - 1)
            if g == 0:
                if s == 1:
                    arrived(g, "own", d)
                if s < FAR - 1:
                    same((g, "p", d, s), xp_full.at[:, zz], ring[d])
                elif s < FAR:
                    same((g, "p", d, s), xp_full.at[d, zz], ring[d])
            else:
                if s < FAR - 1:
                    same((g, "p", d, s), xp_half.at[zz], ring[d])
                elif s < FAR:
                    at = pl.ds(0, cut) if d == 0 else pl.ds(cut, chp - cut)
                    same((g, "p", d, s), xp_half.at[zz, at], ring[d])
            arrived(g, "q", d, s - 1)
            if s < FAR - 1:
                same((g, "q", d, s), xq.at[g, y, zz], ring[d])
            elif s < FAR:
                at = pl.ds(0, cut) if d == 0 else pl.ds(cut, chp - cut)
                same((g, "q", d, s), xq.at[g, y, zz, at], ring[d])
            if s < FAR:
                same((g, "qy", -s if d == 0 else s), xq.at[g, y, zz], other)
        if s == FAR:
            same((g, "qy", FAR), xq.at[g, y, tz(FAR)], other)

    def flatten_w():
        w_flat[:, wide:] = jnp.zeros((2 * ffp, w_flat.shape[1] - wide), BF16)
        w_load.wait()
        w_raw[ff:ffp] = jnp.zeros((ffp - ff, 2, wide), BF16)

        def body(i, _):
            dst = pl.ds(pl.multiple_of(i * 32, 32), 32)
            w_flat[dst, 0:wide] = w_raw[pl.ds(i * 16, 16)].reshape(32, wide)
            return 0

        lax.fori_loop(0, ffp // 16, body, 0)

    def spread_w():
        for j in range(spread // LANES):
            c = LANES * j + iota((PAIR, LANES), 1)
            begin = LANES * j - (chp - ch) * (LANES * j // chp)
            base = begin // LANES * LANES
            p = base + iota((PAIR, LANES), 0)
            owner = c // chp
            pick = one_hot((p == c - (chp - ch) * owner) & (c - chp * owner < ch))
            moved = jnp.dot(w_flat[:, base : base + PAIR], pick, preferred_element_type=F32)
            w_ref[:, LANES * j : LANES * (j + 1)] = moved.astype(BF16)

    def split_w():
        to, at = iota((2 * ffp, 2 * ffp), 0), iota((2 * ffp, 2 * ffp), 1)
        pick = one_hot(at == jnp.where(to < ffp, 2 * to, 2 * (to - ffp) + 1))
        for n in range(spread // PAIR):
            sl = slice(PAIR * n, PAIR * (n + 1))
            w_ref[:, sl] = jnp.dot(pick, w_ref[:, sl], preferred_element_type=F32).astype(BF16)

    def turn_p():
        p_ref[...] = jnp.zeros_like(p_ref)
        p_load.wait()
        for zz in range(NZ):
            for yy in range(NY):
                o = yy * NZ + zz
                p_ref[zz, yy, 0:ch, 0:ff] = p_raw[:, ch * o : ch * (o + 1)].T

    def turn_columns():
        rows_s[...] = jnp.zeros_like(rows_s)
        rows_s[0:2, 0:ff] = bias_ref[...]
        rows_s[2:4, 0:ff] = shift_ref[...]
        for i in range(3):
            for j in range(3):
                n = 4 + 2 * (3 * i + j)
                rows_s[n : n + 2, 0:ff] = taps_ref[i, j]
        cols_s[...] = rows_s[...].T[:ffp]
        for n in range(taps_s.shape[0]):
            taps_s[n] = jnp.broadcast_to(cols_s[:, n : n + 1], (ffp, LANES))

    lane = iota((1, LANES), 1)
    first = lane < HALF
    col = lane % HALF
    left_ok = col > 0
    right_ok = col < HALF - 1
    top_ok = r > 0
    bottom_ok = r < rows - 1

    def expand_p(g):
        if g == 0:
            x = xp_full[...].reshape(spread, LANES)
            pre = jnp.dot(w_ref[...], x, preferred_element_type=F32)
        else:
            x = xp_half[...].reshape(spread // 2, LANES)
            pre = jnp.dot(w_ref[:, : spread // 2], x, preferred_element_type=F32)
            more = jnp.dot(w_ref[:, spread // 2 :], x, preferred_element_type=F32)
            pre = jnp.where(first, pre + pltpu.roll(more, HALF, 1), 0.0)
        for k in range(2):
            value = silu(pre[k * ffp : (k + 1) * ffp] + taps_s[k])
            if g == 1:
                value = jnp.where(first, value, 0.0)
            ec[k * ffp : (k + 1) * ffp, :LANES] = value.astype(BF16)

    def expand_q(g):
        x = xq[g].reshape(spread, LANES)
        pre = jnp.dot(w_ref[...], x, preferred_element_type=F32)
        for k in range(2):
            value = silu(pre[k * ffp : (k + 1) * ffp] + taps_s[k])
            ec[k * ffp : (k + 1) * ffp, LANES:] = value.astype(BF16)

    def restore(g):
        for k in range(2):
            ex[k] = across(ec[k * ffp : (k + 1) * ffp], spot[g])

        def body(i, _):
            at = pl.ds(pl.multiple_of(i * 16, 16), 16)
            for s in range(2):
                sl = slice(s * LANES, (s + 1) * LANES)
                e0, e1 = ex[0, at, sl], ex[1, at, sl]
                dn_out[g, at, sl] = jnp.where(first, pltpu.roll(e0, HALF, 1), e1).astype(BF16)
                up_out[g, at, sl] = jnp.where(first, e0, pltpu.roll(e1, HALF, 1)).astype(BF16)
            return 0

        lax.fori_loop(0, ffp // 16, body, 0)
        start((g, "dn"), dn_out.at[g], dn_in.at[g], below)
        start((g, "up"), up_out.at[g], up_in.at[g], above)

    def convolve(g):
        arrived(g, "dn")
        arrived(g, "up")

        def body(i, _):
            at = pl.ds(pl.multiple_of(i * 16, 16), 16)
            for s in range(2):
                sl = slice(s * LANES, (s + 1) * LANES)
                up = jnp.where(top_ok, dn_in[g, at, sl].astype(F32), 0.0)
                dn = jnp.where(bottom_ok, up_in[g, at, sl].astype(F32), 0.0)
                outs = []
                for k in range(2):
                    mid = ex[k, at, sl]
                    turned = pltpu.roll(mid, HALF, 1)
                    a = up if k == 0 else pltpu.roll(up, HALF, 1)
                    d = pltpu.roll(dn, HALF, 1) if k == 0 else dn
                    seen = [jnp.where(first, a, turned), mid, jnp.where(first, turned, d)]
                    sums = []
                    for j in range(3):
                        n = 4 + 2 * j + k
                        total = taps_s[n, at] * seen[0] + taps_s[n + 6, at] * seen[1]
                        sums.append(total + taps_s[n + 12, at] * seen[2])
                    res = sums[1] + taps_s[2 + k, at]
                    res = res + jnp.where(left_ok, pltpu.roll(sums[0], 1, 1), 0.0)
                    res = res + jnp.where(right_ok, pltpu.roll(sums[2], LANES - 1, 1), 0.0)
                    outs.append(res)
                hid[at, sl] = (outs[0] * silu(outs[1])).astype(BF16)
            return 0

        lax.fori_loop(0, ffp // 16, body, 0)

    def project(g):
        hc[...] = jnp.dot(hid[...], spot[g], preferred_element_type=F32).astype(BF16)
        p = p_ref[...].reshape(spread, ffp)
        part[g] = jnp.dot(p, hc[...], preferred_element_type=F32).reshape(NZ, NY, chp, PAIR)

    def scatter_begin(g):
        for n, d in enumerate(NEAR_ORDER):
            qy_out[g, n] = part[g, tz(d), 1 - y, :, LANES:].astype(BF16)
            start((g, "ry", d), qy_out.at[g, n], qy_in.at[g, n], other)

    def scatter_p(g, s):
        for d in range(2):
            zz = tz(FAR - s if d == 0 else s - FAR)
            if s > 0:
                arrived(g, "rp", d, s - 1)
            if g == 0:
                for yy in range(NY):
                    if s == 0 and yy != d:
                        continue
                    total = part[g, zz, yy, :, :LANES]
                    if s > 1 or (s == 1 and yy == d):
                        total = total + pf_in[d, s - 1, yy].astype(F32)
                    pf_out[d, s, yy] = total.astype(BF16)
                if s == 0:
                    src, dst = pf_out.at[d, s, d], pf_in.at[d, s, d]
                else:
                    src, dst = pf_out.at[d, s], pf_in.at[d, s]
            else:
                near = slice(0, cut) if d == 0 else slice(cut, chp)
                rest = slice(cut, chp) if d == 0 else slice(0, cut)
                for at in (near, rest):
                    if s == 0 and at is rest:
                        continue
                    total = jnp.where(first, part[g, zz, 0, at, :LANES], part[g, zz, 1, at, :LANES])
                    if s > 1 or (s == 1 and at is near):
                        total = total + ph_in[d, s - 1, at].astype(F32)
                    ph_out[d, s, at] = total.astype(BF16)
                if s == 0:
                    src, dst = ph_out.at[d, s, near], ph_in.at[d, s, near]
                else:
                    src, dst = ph_out.at[d, s], ph_in.at[d, s]
            start((g, "rp", d, s), src, dst, ring[d])

    def scatter_q(g, s):
        for d in range(2):
            step = FAR - s if d == 0 else s - FAR
            step = FAR if step == -FAR else step
            n = NEAR_ORDER.index(step)
            if s > 0 or d == 0:
                arrived(g, "ry", step)
            if s > 0:
                arrived(g, "rq", d, s - 1)
            near = slice(0, cut) if d == 0 else slice(cut, chp)
            rest = slice(cut, chp) if d == 0 else slice(0, cut)
            for at in (near, rest):
                if s == 0 and at is rest:
                    continue
                total = part[g, tz(step), y, at, LANES:] + qy_in[g, n, at].astype(F32)
                if s > 1 or (s == 1 and at is near):
                    total = total + qz_in[g, d, s - 1, at].astype(F32)
                qz_out[g, d, s, at] = total.astype(BF16)
            if s == 0:
                src, dst = qz_out.at[g, d, s, near], qz_in.at[g, d, s, near]
            else:
                src, dst = qz_out.at[g, d, s], qz_in.at[g, d, s]
            start((g, "rq", d, s), src, dst, ring[d])

    last = FAR - 1

    def scatter_pair(g):
        for d in range(2):
            arrived(g, "rp", d, last)
        if g == 0:
            total = part[g, z, 1 - y, :, :LANES]
            total = total + pf_in[0, last, 1 - y].astype(F32) + pf_in[1, last, 1 - y].astype(F32)
            py_out[g] = total.astype(BF16)
        else:
            py_out[g] = half_sum(1).astype(BF16)
        start((g, "py"), py_out.at[g], py_in.at[g], other)

    def half_sum(g):
        total = jnp.where(first, part[g, z, 0, :, :LANES], part[g, z, 1, :, :LANES])
        return total + ph_in[0, last].astype(F32) + ph_in[1, last].astype(F32)

    def finish_q(g):
        for d in range(2):
            arrived(g, "rq", d, last)
        arrived(g, "ry", 0)
        n = NEAR_ORDER.index(0)
        total = part[g, z, y, :, LANES:] + qy_in[g, n].astype(F32)
        return total + qz_in[g, 0, last].astype(F32) + qz_in[g, 1, last].astype(F32)

    def finish_p(g):
        if g == 0:
            total = part[g, z, y, :, :LANES]
            total = total + pf_in[0, last, y].astype(F32) + pf_in[1, last, y].astype(F32)
        else:
            total = half_sum(1)
        arrived(g, "py")
        return total + py_in[g].astype(F32)

    def restored(g):
        q = finish_q(g).astype(BF16)
        p = finish_p(g).astype(BF16)
        return across(place[g, :, :LANES], p) + across(place[g, :, LANES:], q)

    gather_begin(0)
    turn_columns()
    gather_pair(0)
    flatten_w()
    gather_step(0, 1)
    gather_begin(1)
    spread_w()
    gather_step(0, 2)
    gather_pair(1)
    split_w()
    gather_step(0, 3)
    gather_step(1, 1)
    make_spot()
    gather_step(0, 4)
    gather_step(1, 2)
    expand_p(0)
    for d in NEAR_ORDER:
        arrived(0, "qy", d)
    expand_q(0)
    restore(0)
    gather_step(1, 3)
    turn_p()
    gather_step(1, 4)
    convolve(0)
    project(0)
    scatter_begin(0)
    scatter_p(0, 0)
    scatter_q(0, 0)
    expand_p(1)
    for d in NEAR_ORDER:
        arrived(1, "qy", d)
    expand_q(1)
    scatter_p(0, 1)
    scatter_q(0, 1)
    restore(1)
    scatter_p(0, 2)
    scatter_q(0, 2)
    convolve(1)
    project(1)
    scatter_begin(1)
    scatter_p(1, 0)
    scatter_p(0, 3)
    scatter_q(0, 3)
    scatter_q(1, 0)
    scatter_p(1, 1)
    scatter_q(1, 1)
    scatter_pair(0)
    scatter_p(1, 2)
    scatter_q(1, 2)
    acc = restored(0)
    scatter_p(1, 3)
    scatter_q(1, 3)
    scatter_pair(1)
    acc = acc + restored(1)
    out_ref[...] = acc[:, :ch].astype(BF16).reshape(out_ref.shape)
    for c in pending.values():
        c.wait_send()


def on_device(
    row_devices,
    latents,
    clip_height,
    clip_width,
    expand_weight,
    expand_bias,
    depth_weight,
    depth_bias,
    project_weight,
):
    batch, row_count, col_count, ch = latents.shape
    ff = expand_bias.shape[1]
    assert batch == 4 and row_count == 2 and col_count == HALF
    chp, ffp = ceil_to(ch, 16), ceil_to(ff, 16)
    spread = NY * NZ * chp

    vmem = pl.BlockSpec(memory_space=pltpu.VMEM)
    smem = pl.BlockSpec(memory_space=pltpu.SMEM)
    hbm = pl.BlockSpec(memory_space=pl.ANY)
    scratch = [
        pltpu.VMEM((ffp, 2, NY * NZ * ch), BF16),
        pltpu.VMEM((2 * ffp, spread + LANES), BF16),
        pltpu.VMEM((2 * ffp, spread), BF16),
        pltpu.VMEM((ff, NY * NZ * ch), BF16),
        pltpu.VMEM((NZ, NY, chp, ffp), BF16),
        pltpu.VMEM((LANES, ceil_to(ffp, LANES)), F32),
        pltpu.VMEM((ffp, LANES), F32),
        pltpu.VMEM((22, ffp, LANES), F32),
        pltpu.VMEM((2, batch * LANES, PAIR), BF16),
        pltpu.VMEM((2, PAIR, PAIR), BF16),
        pltpu.VMEM((NY, NZ, chp, LANES), BF16),
        pltpu.VMEM((NZ, chp, LANES), BF16),
        pltpu.VMEM((2, NY, NZ, chp, LANES), BF16),
        pltpu.VMEM((chp, LANES), BF16),
        pltpu.VMEM((chp, LANES), BF16),
        pltpu.VMEM((2 * ffp, PAIR), BF16),
        pltpu.VMEM((2, ffp, PAIR), F32),
        pltpu.VMEM((2, ffp, PAIR), BF16),
        pltpu.VMEM((2, ffp, PAIR), BF16),
        pltpu.VMEM((2, ffp, PAIR), BF16),
        pltpu.VMEM((2, ffp, PAIR), BF16),
        pltpu.VMEM((ffp, PAIR), BF16),
        pltpu.VMEM((ffp, PAIR), BF16),
        pltpu.VMEM((2, NZ, NY, chp, PAIR), F32),
        pltpu.VMEM((2, FAR, NY, chp, LANES), BF16),
        pltpu.VMEM((2, FAR, NY, chp, LANES), BF16),
        pltpu.VMEM((2, FAR, chp, LANES), BF16),
        pltpu.VMEM((2, FAR, chp, LANES), BF16),
        pltpu.VMEM((2, 2, FAR, chp, LANES), BF16),
        pltpu.VMEM((2, 2, FAR, chp, LANES), BF16),
        pltpu.VMEM((2, NZ, chp, LANES), BF16),
        pltpu.VMEM((2, NZ, chp, LANES), BF16),
        pltpu.VMEM((2, chp, LANES), BF16),
        pltpu.VMEM((2, chp, LANES), BF16),
        pltpu.SemaphoreType.DMA((2,)),
        pltpu.SemaphoreType.DMA((128,)),
        pltpu.SemaphoreType.DMA((128,)),
    ]
    return pl.pallas_call(
        functools.partial(kernel, row_devices),
        out_shape=jax.ShapeDtypeStruct(latents.shape, BF16),
        in_specs=[vmem, smem, smem, hbm, vmem, vmem, vmem, hbm],
        out_specs=vmem,
        scratch_shapes=scratch,
        compiler_params=pltpu.CompilerParams(
            collective_id=0, has_side_effects=True, vmem_limit_bytes=60 * 1024 * 1024
        ),
    )(
        latents,
        clip_height,
        clip_width,
        expand_weight.transpose(2, 0, 1),
        expand_bias,
        depth_weight,
        depth_bias,
        project_weight,
    )


def solution(mesh):
    in_specs = (
        P(None, "row", None, "tensor"),
        P(),
        P(),
        P(None, None, "tensor"),
        P(None, "tensor"),
        P(None, None, None, "tensor"),
        P(None, "tensor"),
        P("tensor", None),
    )
    return jax.shard_map(
        functools.partial(on_device, mesh.shape["row"]),
        mesh=mesh,
        in_specs=in_specs,
        out_specs=P(None, "row", None, "tensor"),
        check_vma=False,
    )
```

time: 280 us -> 86.5 us (0.31)
  waiting for transfers between devices: 236 us -> 0 us
  Pallas kernels: 0 us -> 83.3 us
  between operations: 14.2 us -> 0.01 us
  matrix products: 9.88 us -> 0 us
  starting transfers between devices: 9.22 us -> 0 us
  other arithmetic: 6.2 us -> 0 us
    unnamed x3 -> x0, waiting for transfers between devices: 152 us -> none
    pallas_call x0 -> x1, Pallas kernels: none -> 83.3 us  [on_device(): pl.pallas_call(functools.partial(kernel, row_devices), out_shape=jax.Shap...]
    all_gather x1 -> x0, waiting for transfers between devices: 78.3 us -> none  [on_device(): lax.all_gather(latents, 'tensor', axis=3, tiled=True)]
    dot_general x2 -> x0, matrix products: 9.88 us -> none  [the longest x1 6.23 us: on_device(): jnp.einsum('brcd,kdf->brckf', lax.all_gather(latents, 'tensor', axis=3, t...]
    ppermute x2 -> x0, starting transfers between devices: 9.18 us -> none  [the longest x1 7.26 us: padded_2(): lax.ppermute(head, axis, [((i + 1) % count, i) for i in range(ends)])]
    ppermute x2 -> x0, waiting for transfers between devices: 5.23 us -> none  [the longest x1 3.48 us: padded_2(): lax.ppermute(tail, axis, [(i, (i + 1) % count) for i in range(ends)])]
  transfers between devices with their start and end apart: 4 -> 0, of which waited for: 4 -> 0; matrix products, arithmetic and copies ran while one was open for 1% -> 0% of each run, Pallas kernels for 0% -> 0%
where the time goes in v3:
time: 86.5 us; the launch traced here: 85 us
  Pallas kernels  83.3 us (96%)
  local copies, waits for them, and re-layouts  1.67 us (2%)
    pallas_call x1, Pallas kernels, on_device(): pl.pallas_call(functools.partial(kernel, row_devices), out_shape=jax.Shap...  83.3 us

profile of v3, /device:TPU:16, one launch (start us, length us, event | category | flops | bytes accessed | tf_op | source)
XLA Modules:
  0.0 85.0 jit_solution(11244606563827305766)
XLA Ops:
  0.0 83.3 %shard_map.82 = bf16[4,2,64,140]{3,2,1,0:T(8,128)(2,1)} custom-call(bf16[4,2,64,140]{3,2,1,0:T(8,128)(2,1)} %x_ref.1, s32[4]{0:T(128)} %height_ref.1, s32[4]{0:T(128)} %width_ref.1, bf16[350,2,2240]{2,1,0:T(2,128)(2,1)} %bitcast.1, f32[2,350]{1,0:T(2,128)} %bias_ref.1, f32[3,3,2,350]{3,2,1,0:T(2,128)} %taps_ref.1, f32[2,350]{1,0:T(2,128)} %shift_ref.1, ...), custom_call_target="tpu_custom_call" | custom-call | tf_op jit(solution)/shard_map/pallas_call | solution.py:596
  83.3 1.7 %copy.10 = bf16[4,2,64,140]{3,2,1,0:T(8,128)(2,1)} copy(bf16[4,2,64,140]{3,2,1,0:T(8,128)(2,1)} %shard_map.82) | data formatting | bytes 286720

commit v4 on v3

--- a/solution.py
+++ b/solution.py
@@ -91,7 +91,7 @@
     t = lax.axis_index("tensor")
     y, z = t // NZ, t % NZ
     clips, row_count, col_count, ch = x_ref.shape
-    ff, ffp, chp = bias_ref.shape[1], ex.shape[1], xq.shape[3]
+    ff, ffp, chp = bias_ref.shape[1], ex.shape[2], xq.shape[3]
     wide, spread = NY * NZ * ch, NY * NZ * chp
     cut = ceil_to(chp // 2, 16)
 
@@ -323,18 +323,18 @@
 
     def restore(g):
         for k in range(2):
-            ex[k] = across(ec[k * ffp : (k + 1) * ffp], spot[g])
+            ex[g, k] = across(ec[k * ffp : (k + 1) * ffp], spot[g])
 
         def body(i, _):
             at = pl.ds(pl.multiple_of(i * 16, 16), 16)
             for s in range(2):
                 sl = slice(s * LANES, (s + 1) * LANES)
-                e0, e1 = ex[0, at, sl], ex[1, at, sl]
+                e0, e1 = ex[g, 0, at, sl], ex[g, 1, at, sl]
                 dn_out[g, at, sl] = jnp.where(first, pltpu.roll(e0, HALF, 1), e1).astype(BF16)
                 up_out[g, at, sl] = jnp.where(first, e0, pltpu.roll(e1, HALF, 1)).astype(BF16)
             return 0
 
-        lax.fori_loop(0, ffp // 16, body, 0)
+        lax.fori_loop(0, ffp // 16, body, 0, unroll=11)
         start((g, "dn"), dn_out.at[g], dn_in.at[g], below)
         start((g, "up"), up_out.at[g], up_in.at[g], above)
 
@@ -350,7 +350,7 @@
                 dn = jnp.where(bottom_ok, up_in[g, at, sl].astype(F32), 0.0)
                 outs = []
                 for k in range(2):
-                    mid = ex[k, at, sl]
+                    mid = ex[g, k, at, sl]
                     turned = pltpu.roll(mid, HALF, 1)
                     a = up if k == 0 else pltpu.roll(up, HALF, 1)
                     d = pltpu.roll(dn, HALF, 1) if k == 0 else dn
@@ -367,7 +367,7 @@
                 hid[at, sl] = (outs[0] * silu(outs[1])).astype(BF16)
             return 0
 
-        lax.fori_loop(0, ffp // 16, body, 0)
+        lax.fori_loop(0, ffp // 16, body, 0, unroll=2)
 
     def project(g):
         hc[...] = jnp.dot(hid[...], spot[g], preferred_element_type=F32).astype(BF16)
@@ -476,58 +476,50 @@
         return across(place[g, :, :LANES], p) + across(place[g, :, LANES:], q)
 
     gather_begin(0)
+    gather_begin(1)
     turn_columns()
     gather_pair(0)
+    gather_pair(1)
     flatten_w()
     gather_step(0, 1)
-    gather_begin(1)
+    gather_step(1, 1)
     spread_w()
     gather_step(0, 2)
-    gather_pair(1)
+    gather_step(1, 2)
     split_w()
     gather_step(0, 3)
-    gather_step(1, 1)
+    gather_step(1, 3)
     make_spot()
+    turn_p()
     gather_step(0, 4)
-    gather_step(1, 2)
+    gather_step(1, 4)
     expand_p(0)
     for d in NEAR_ORDER:
         arrived(0, "qy", d)
     expand_q(0)
     restore(0)
-    gather_step(1, 3)
-    turn_p()
-    gather_step(1, 4)
+    expand_p(1)
+    for d in NEAR_ORDER:
+        arrived(1, "qy", d)
+    expand_q(1)
+    restore(1)
     convolve(0)
     project(0)
     scatter_begin(0)
     scatter_p(0, 0)
     scatter_q(0, 0)
-    expand_p(1)
-    for d in NEAR_ORDER:
-        arrived(1, "qy", d)
-    expand_q(1)
-    scatter_p(0, 1)
-    scatter_q(0, 1)
-    restore(1)
-    scatter_p(0, 2)
-    scatter_q(0, 2)
     convolve(1)
     project(1)
     scatter_begin(1)
     scatter_p(1, 0)
-    scatter_p(0, 3)
-    scatter_q(0, 3)
     scatter_q(1, 0)
-    scatter_p(1, 1)
-    scatter_q(1, 1)
+    for s in range(1, FAR):
+        for g in range(2):
+            scatter_p(g, s)
+            scatter_q(g, s)
     scatter_pair(0)
-    scatter_p(1, 2)
-    scatter_q(1, 2)
+    scatter_pair(1)
     acc = restored(0)
-    scatter_p(1, 3)
-    scatter_q(1, 3)
-    scatter_pair(1)
     acc = acc + restored(1)
     out_ref[...] = acc[:, :ch].astype(BF16).reshape(out_ref.shape)
     for c in pending.values():
@@ -571,7 +563,7 @@
         pltpu.VMEM((chp, LANES), BF16),
         pltpu.VMEM((chp, LANES), BF16),
         pltpu.VMEM((2 * ffp, PAIR), BF16),
-        pltpu.VMEM((2, ffp, PAIR), F32),
+        pltpu.VMEM((2, 2, ffp, PAIR), F32),
         pltpu.VMEM((2, ffp, PAIR), BF16),
         pltpu.VMEM((2, ffp, PAIR), BF16),
         pltpu.VMEM((2, ffp, PAIR), BF16),

time: 86.5 us -> 72.4 us (0.84); the launches traced: 85 us -> 72.3 us
  Pallas kernels: 83.3 us -> 70.6 us
    pallas_call x1, Pallas kernels: 83.3 us -> 70.6 us  [on_device(): pl.pallas_call(functools.partial(kernel, row_devices), out_shape=jax.Shap...]
where the time goes in v4:
time: 72.4 us; the launch traced here: 72.3 us
  Pallas kernels  70.6 us (98%)
  local copies, waits for them, and re-layouts  1.67 us (2%)
    pallas_call x1, Pallas kernels, on_device(): pl.pallas_call(functools.partial(kernel, row_devices), out_shape=jax.Shap...  70.6 us
    unnamed x1, local copies, waits for them, and re-layouts  1.67 us

profile of v4, /device:TPU:16, one launch (start us, length us, event | category | flops | bytes accessed | tf_op | source)
XLA Modules:
  0.0 72.3 jit_solution(15956587466222041266)
XLA Ops:
  0.0 70.6 %shard_map.82 = bf16[4,2,64,140]{3,2,1,0:T(8,128)(2,1)} custom-call(bf16[4,2,64,140]{3,2,1,0:T(8,128)(2,1)} %x_ref.1, s32[4]{0:T(128)} %height_ref.1, s32[4]{0:T(128)} %width_ref.1, bf16[350,2,2240]{2,1,0:T(2,128)(2,1)} %bitcast.1, f32[2,350]{1,0:T(2,128)} %bias_ref.1, f32[3,3,2,350]{3,2,1,0:T(2,128)} %taps_ref.1, f32[2,350]{1,0:T(2,128)} %shift_ref.1, ...), custom_call_target="tpu_custom_call" | custom-call | tf_op jit(solution)/shard_map/pallas_call | solution.py:588
  70.6 1.7 %copy.10 = bf16[4,2,64,140]{3,2,1,0:T(8,128)(2,1)} copy(bf16[4,2,64,140]{3,2,1,0:T(8,128)(2,1)} %shard_map.82) | data formatting | bytes 286720

commit v5 on v4

--- a/solution.py
+++ b/solution.py
@@ -15,7 +15,8 @@
 PAIR = 2 * LANES
 BF16 = jnp.bfloat16
 F32 = jnp.float32
-NEAR_ORDER = (4, 3, -3, 2, -2, 1, -1, 0)
+NEAR_ORDER = (3, -3, 4, 2, -2, 1, -1, 0)
+STEPS = FAR - 1
 
 
 def ceil_to(n, m):
@@ -66,6 +67,8 @@
     hx_in,
     ec,
     ex,
+    turned,
+    sums,
     dn_out,
     up_out,
     dn_in,
@@ -99,6 +102,7 @@
         return (z + NZ + step) % NZ
 
     ring = ({"tensor": y * NZ + tz(1)}, {"tensor": y * NZ + tz(-1)})
+    ring2 = ({"tensor": y * NZ + tz(2)}, {"tensor": y * NZ + tz(-2)})
     other = {"tensor": (1 - y) * NZ + z}
     above = {"row": (r + rows - 1) % rows}
     below = {"row": (r + 1) % rows}
@@ -109,7 +113,7 @@
     p_load.start()
 
     barrier = pltpu.get_barrier_semaphore()
-    for target in ring + (other, above, below):
+    for target in ring + ring2 + (other, above, below):
         pl.semaphore_signal(barrier, inc=1, device_id=target, device_id_type=MESH)
 
     pending = {}
@@ -190,7 +194,7 @@
         xq[g, y, z, 0:ch] = block[:, LANES:]
         xq[g, y, z, ch:chp] = empty
 
-    pl.semaphore_wait(barrier, 5)
+    pl.semaphore_wait(barrier, 7)
 
     def gather_begin(g):
         if g == 0:
@@ -213,33 +217,35 @@
             for d in range(2):
                 same((g, "p", d, 0), xp_half.at[z], ring[d])
 
+    def cut_at(d):
+        return pl.ds(0, cut) if d == 0 else pl.ds(cut, chp - cut)
+
     def gather_step(g, s):
         for d in range(2):
             zz = tz(-s if d == 0 else s)
             arrived(g, "p", d, s - 1)
-            if g == 0:
-                if s == 1:
-                    arrived(g, "own", d)
-                if s < FAR - 1:
-                    same((g, "p", d, s), xp_full.at[:, zz], ring[d])
-                elif s < FAR:
-                    same((g, "p", d, s), xp_full.at[d, zz], ring[d])
-            else:
-                if s < FAR - 1:
-                    same((g, "p", d, s), xp_half.at[zz], ring[d])
-                elif s < FAR:
-                    at = pl.ds(0, cut) if d == 0 else pl.ds(cut, chp - cut)
-                    same((g, "p", d, s), xp_half.at[zz, at], ring[d])
+            if g == 0 and s == 1:
+                arrived(g, "own", d)
+            if s < STEPS:
+                src = xp_full.at[:, zz] if g == 0 else xp_half.at[zz]
+                same((g, "p", d, s), src, ring[d])
+            if s == 2:
+                src = xp_full.at[d, zz] if g == 0 else xp_half.at[zz, cut_at(d)]
+                same((g, "pf", d), src, ring2[d])
+        for d in range(2):
+            zz = tz(-s if d == 0 else s)
             arrived(g, "q", d, s - 1)
-            if s < FAR - 1:
+            if s < STEPS:
                 same((g, "q", d, s), xq.at[g, y, zz], ring[d])
-            elif s < FAR:
-                at = pl.ds(0, cut) if d == 0 else pl.ds(cut, chp - cut)
-                same((g, "q", d, s), xq.at[g, y, zz, at], ring[d])
-            if s < FAR:
-                same((g, "qy", -s if d == 0 else s), xq.at[g, y, zz], other)
-        if s == FAR:
+            if s == 2:
+                same((g, "qf", d), xq.at[g, y, zz, cut_at(d)], ring2[d])
+            same((g, "qy", -s if d == 0 else s), xq.at[g, y, zz], other)
+        if s == STEPS:
+            for d in range(2):
+                arrived(g, "qf", d)
             same((g, "qy", FAR), xq.at[g, y, tz(FAR)], other)
+            for d in range(2):
+                arrived(g, "pf", d)
 
     def flatten_w():
         w_flat[:, wide:] = jnp.zeros((2 * ffp, w_flat.shape[1] - wide), BF16)
@@ -288,16 +294,25 @@
                 n = 4 + 2 * (3 * i + j)
                 rows_s[n : n + 2, 0:ff] = taps_ref[i, j]
         cols_s[...] = rows_s[...].T[:ffp]
-        for n in range(taps_s.shape[0]):
-            taps_s[n] = jnp.broadcast_to(cols_s[:, n : n + 1], (ffp, LANES))
+
+        def wide_col(n):
+            return jnp.broadcast_to(cols_s[:, n : n + 1], (ffp, LANES))
+
+        for n in range(4):
+            taps_s[n] = wide_col(n)
+        for m in range(6):
+            above_tap, below_tap = wide_col(4 + m), wide_col(16 + m)
+            taps_s[4 + m] = wide_col(10 + m)
+            taps_s[10 + m] = jnp.where(first, below_tap, above_tap)
+            taps_s[16 + m] = jnp.where(first, above_tap, below_tap)
 
     lane = iota((1, LANES), 1)
     first = lane < HALF
     col = lane % HALF
     left_ok = col > 0
     right_ok = col < HALF - 1
-    top_ok = r > 0
-    bottom_ok = r < rows - 1
+    edge_row = row_count * r + jnp.where(first, -1, row_count)
+    edge_ok = (edge_row >= 0) & (edge_row < rows * row_count)
 
     def expand_p(g):
         if g == 0:
@@ -330,8 +345,11 @@
             for s in range(2):
                 sl = slice(s * LANES, (s + 1) * LANES)
                 e0, e1 = ex[g, 0, at, sl], ex[g, 1, at, sl]
-                dn_out[g, at, sl] = jnp.where(first, pltpu.roll(e0, HALF, 1), e1).astype(BF16)
-                up_out[g, at, sl] = jnp.where(first, e0, pltpu.roll(e1, HALF, 1)).astype(BF16)
+                t0, t1 = pltpu.roll(e0, HALF, 1), pltpu.roll(e1, HALF, 1)
+                turned[g, 0, at, sl] = t0
+                turned[g, 1, at, sl] = t1
+                dn_out[g, at, sl] = jnp.where(first, t0, e1).astype(BF16)
+                up_out[g, at, sl] = jnp.where(first, e0, t1).astype(BF16)
             return 0
 
         lax.fori_loop(0, ffp // 16, body, 0, unroll=11)
@@ -339,6 +357,21 @@
         start((g, "up"), up_out.at[g], up_in.at[g], above)
 
     def convolve(g):
+        def body(i, _):
+            at = pl.ds(pl.multiple_of(i * 16, 16), 16)
+            for k in range(2):
+                for s in range(2):
+                    sl = slice(s * LANES, (s + 1) * LANES)
+                    mid, swap = ex[g, k, at, sl], turned[g, k, at, sl]
+                    for j in range(3):
+                        n = 2 * j + k
+                        total = taps_s[4 + n, at] * mid + taps_s[10 + n, at] * swap
+                        sums[g, j, k, at, sl] = total
+            return 0
+
+        lax.fori_loop(0, ffp // 16, body, 0, unroll=2)
+
+    def complete(g):
         arrived(g, "dn")
         arrived(g, "up")
 
@@ -346,23 +379,18 @@
             at = pl.ds(pl.multiple_of(i * 16, 16), 16)
             for s in range(2):
                 sl = slice(s * LANES, (s + 1) * LANES)
-                up = jnp.where(top_ok, dn_in[g, at, sl].astype(F32), 0.0)
-                dn = jnp.where(bottom_ok, up_in[g, at, sl].astype(F32), 0.0)
+                dn, up = dn_in[g, at, sl].astype(F32), up_in[g, at, sl].astype(F32)
+                edges = (
+                    jnp.where(first, dn, pltpu.roll(up, HALF, 1)),
+                    jnp.where(first, pltpu.roll(dn, HALF, 1), up),
+                )
                 outs = []
                 for k in range(2):
-                    mid = ex[g, k, at, sl]
-                    turned = pltpu.roll(mid, HALF, 1)
-                    a = up if k == 0 else pltpu.roll(up, HALF, 1)
-                    d = pltpu.roll(dn, HALF, 1) if k == 0 else dn
-                    seen = [jnp.where(first, a, turned), mid, jnp.where(first, turned, d)]
-                    sums = []
-                    for j in range(3):
-                        n = 4 + 2 * j + k
-                        total = taps_s[n, at] * seen[0] + taps_s[n + 6, at] * seen[1]
-                        sums.append(total + taps_s[n + 12, at] * seen[2])
-                    res = sums[1] + taps_s[2 + k, at]
-                    res = res + jnp.where(left_ok, pltpu.roll(sums[0], 1, 1), 0.0)
-                    res = res + jnp.where(right_ok, pltpu.roll(sums[2], LANES - 1, 1), 0.0)
+                    edge = jnp.where(edge_ok, edges[k], 0.0)
+                    got = [sums[g, j, k, at, sl] + taps_s[16 + 2 * j + k, at] * edge for j in range(3)]
+                    res = got[1] + taps_s[2 + k, at]
+                    res = res + jnp.where(left_ok, pltpu.roll(got[0], 1, 1), 0.0)
+                    res = res + jnp.where(right_ok, pltpu.roll(got[2], LANES - 1, 1), 0.0)
                     outs.append(res)
                 hid[at, sl] = (outs[0] * silu(outs[1])).astype(BF16)
             return 0
@@ -379,64 +407,79 @@
             qy_out[g, n] = part[g, tz(d), 1 - y, :, LANES:].astype(BF16)
             start((g, "ry", d), qy_out.at[g, n], qy_in.at[g, n], other)
 
+    def cut_of(d):
+        return slice(0, cut) if d == 0 else slice(cut, chp)
+
+    def half_block(zz, at):
+        return jnp.where(first, part[1, zz, 0, at, :LANES], part[1, zz, 1, at, :LANES])
+
     def scatter_p(g, s):
         for d in range(2):
-            zz = tz(FAR - s if d == 0 else s - FAR)
+            zz = tz(STEPS - s if d == 0 else s - STEPS)
+            near = cut_of(d)
+            if s == 0:
+                if g == 0:
+                    pf_out[d, STEPS, d] = part[0, tz(FAR), d, :, :LANES].astype(BF16)
+                    src, dst = pf_out.at[d, STEPS, d], pf_in.at[d, STEPS, d]
+                else:
+                    ph_out[d, STEPS, near] = half_block(tz(FAR), near).astype(BF16)
+                    src, dst = ph_out.at[d, STEPS, near], ph_in.at[d, STEPS, near]
+                start((g, "rpf", d), src, dst, ring2[d])
             if s > 0:
                 arrived(g, "rp", d, s - 1)
+            if s == 1:
+                arrived(g, "rpf", d)
             if g == 0:
                 for yy in range(NY):
-                    if s == 0 and yy != d:
-                        continue
-                    total = part[g, zz, yy, :, :LANES]
-                    if s > 1 or (s == 1 and yy == d):
+                    total = part[0, zz, yy, :, :LANES]
+                    if s > 0:
                         total = total + pf_in[d, s - 1, yy].astype(F32)
+                    if s == 1 and yy == d:
+                        total = total + pf_in[d, STEPS, yy].astype(F32)
                     pf_out[d, s, yy] = total.astype(BF16)
-                if s == 0:
-                    src, dst = pf_out.at[d, s, d], pf_in.at[d, s, d]
-                else:
-                    src, dst = pf_out.at[d, s], pf_in.at[d, s]
+                src, dst = pf_out.at[d, s], pf_in.at[d, s]
             else:
-                near = slice(0, cut) if d == 0 else slice(cut, chp)
-                rest = slice(cut, chp) if d == 0 else slice(0, cut)
-                for at in (near, rest):
-                    if s == 0 and at is rest:
-                        continue
-                    total = jnp.where(first, part[g, zz, 0, at, :LANES], part[g, zz, 1, at, :LANES])
-                    if s > 1 or (s == 1 and at is near):
+                for e in range(2):
+                    at = cut_of(e)
+                    total = half_block(zz, at)
+                    if s > 0:
                         total = total + ph_in[d, s - 1, at].astype(F32)
+                    if s == 1 and e == d:
+                        total = total + ph_in[d, STEPS, at].astype(F32)
                     ph_out[d, s, at] = total.astype(BF16)
-                if s == 0:
-                    src, dst = ph_out.at[d, s, near], ph_in.at[d, s, near]
-                else:
-                    src, dst = ph_out.at[d, s], ph_in.at[d, s]
+                src, dst = ph_out.at[d, s], ph_in.at[d, s]
             start((g, "rp", d, s), src, dst, ring[d])
+
+    def q_block(g, step, at):
+        n = NEAR_ORDER.index(step)
+        return part[g, tz(step), y, at, LANES:] + qy_in[g, n, at].astype(F32)
 
     def scatter_q(g, s):
         for d in range(2):
-            step = FAR - s if d == 0 else s - FAR
-            step = FAR if step == -FAR else step
-            n = NEAR_ORDER.index(step)
-            if s > 0 or d == 0:
-                arrived(g, "ry", step)
+            step = STEPS - s if d == 0 else s - STEPS
+            arrived(g, "ry", step)
             if s > 0:
                 arrived(g, "rq", d, s - 1)
-            near = slice(0, cut) if d == 0 else slice(cut, chp)
-            rest = slice(cut, chp) if d == 0 else slice(0, cut)
-            for at in (near, rest):
-                if s == 0 and at is rest:
-                    continue
-                total = part[g, tz(step), y, at, LANES:] + qy_in[g, n, at].astype(F32)
-                if s > 1 or (s == 1 and at is near):
+            if s == 1:
+                arrived(g, "rqf", d)
+            for e in range(2):
+                at = cut_of(e)
+                total = q_block(g, step, at)
+                if s > 0:
                     total = total + qz_in[g, d, s - 1, at].astype(F32)
+                if s == 1 and e == d:
+                    total = total + qz_in[g, d, STEPS, at].astype(F32)
                 qz_out[g, d, s, at] = total.astype(BF16)
-            if s == 0:
-                src, dst = qz_out.at[g, d, s, near], qz_in.at[g, d, s, near]
-            else:
-                src, dst = qz_out.at[g, d, s], qz_in.at[g, d, s]
-            start((g, "rq", d, s), src, dst, ring[d])
-
-    last = FAR - 1
+            start((g, "rq", d, s), qz_out.at[g, d, s], qz_in.at[g, d, s], ring[d])
+        if s == 0:
+            arrived(g, "ry", FAR)
+            for d in range(2):
+                at = cut_of(d)
+                qz_out[g, d, STEPS, at] = q_block(g, FAR, at).astype(BF16)
+                src, dst = qz_out.at[g, d, STEPS, at], qz_in.at[g, d, STEPS, at]
+                start((g, "rqf", d), src, dst, ring2[d])
+
+    last = STEPS - 1
 
     def scatter_pair(g):
         for d in range(2):
@@ -487,12 +530,10 @@
     gather_step(0, 2)
     gather_step(1, 2)
     split_w()
+    make_spot()
+    turn_p()
     gather_step(0, 3)
     gather_step(1, 3)
-    make_spot()
-    turn_p()
-    gather_step(0, 4)
-    gather_step(1, 4)
     expand_p(0)
     for d in NEAR_ORDER:
         arrived(0, "qy", d)
@@ -504,16 +545,18 @@
     expand_q(1)
     restore(1)
     convolve(0)
+    convolve(1)
+    complete(0)
     project(0)
     scatter_begin(0)
     scatter_p(0, 0)
     scatter_q(0, 0)
-    convolve(1)
+    complete(1)
     project(1)
     scatter_begin(1)
     scatter_p(1, 0)
     scatter_q(1, 0)
-    for s in range(1, FAR):
+    for s in range(1, STEPS):
         for g in range(2):
             scatter_p(g, s)
             scatter_q(g, s)
@@ -564,6 +607,8 @@
         pltpu.VMEM((chp, LANES), BF16),
         pltpu.VMEM((2 * ffp, PAIR), BF16),
         pltpu.VMEM((2, 2, ffp, PAIR), F32),
+        pltpu.VMEM((2, 2, ffp, PAIR), F32),
+        pltpu.VMEM((2, 3, 2, ffp, PAIR), F32),
         pltpu.VMEM((2, ffp, PAIR), BF16),
         pltpu.VMEM((2, ffp, PAIR), BF16),
         pltpu.VMEM((2, ffp, PAIR), BF16),

time: 72.4 us -> 71.8 us (level); the launches traced: 72.3 us -> 70.9 us
  Pallas kernels: 70.6 us -> 69.2 us
    pallas_call x1, Pallas kernels: 70.6 us -> 69.2 us  [on_device(): pl.pallas_call(functools.partial(kernel, row_devices), out_shape=jax.Shap...]
where the time goes in v5:
time: 71.8 us; the launch traced here: 70.9 us
  Pallas kernels  69.2 us (96%)
  local copies, waits for them, and re-layouts  1.67 us (2%)
    pallas_call x1, Pallas kernels, on_device(): pl.pallas_call(functools.partial(kernel, row_devices), out_shape=jax.Shap...  69.2 us
    unnamed x1, local copies, waits for them, and re-layouts  1.67 us

profile of v5, /device:TPU:16, one launch (start us, length us, event | category | flops | bytes accessed | tf_op | source)
XLA Modules:
  0.0 70.9 jit_solution(561984790676489142)
XLA Ops:
  0.0 69.2 %shard_map.82 = bf16[4,2,64,140]{3,2,1,0:T(8,128)(2,1)} custom-call(bf16[4,2,64,140]{3,2,1,0:T(8,128)(2,1)} %x_ref.1, s32[4]{0:T(128)} %height_ref.1, s32[4]{0:T(128)} %width_ref.1, bf16[350,2,2240]{2,1,0:T(2,128)(2,1)} %bitcast.1, f32[2,350]{1,0:T(2,128)} %bias_ref.1, f32[3,3,2,350]{3,2,1,0:T(2,128)} %taps_ref.1, f32[2,350]{1,0:T(2,128)} %shift_ref.1, ...), custom_call_target="tpu_custom_call" | custom-call | tf_op jit(solution)/shard_map/pallas_call | solution.py:633
  69.2 1.7 %copy.10 = bf16[4,2,64,140]{3,2,1,0:T(8,128)(2,1)} copy(bf16[4,2,64,140]{3,2,1,0:T(8,128)(2,1)} %shard_map.82) | data formatting | bytes 286720

commit v6 on v5

--- a/solution.py
+++ b/solution.py
@@ -24,7 +24,8 @@
 
 
 def silu(v):
-    return v / (1.0 + jnp.exp(-v))
+    h = 0.5 * v
+    return h + h * jnp.tanh(h)
 
 
 def iota(shape, dim):
@@ -205,7 +206,6 @@
             start((g, "y"), hx_out, hx_in, other)
         for d in range(2):
             same((g, "q", d, 0), xq.at[g, y, z], ring[d])
-        same((g, "qy", 0), xq.at[g, y, z], other)
 
     def gather_pair(g):
         arrived(g, "y")
@@ -216,6 +216,7 @@
             xp_half[z] = hx_out[...] + hx_in[...]
             for d in range(2):
                 same((g, "p", d, 0), xp_half.at[z], ring[d])
+        same((g, "qy", 0), xq.at[g, y, z], other)
 
     def cut_at(d):
         return pl.ds(0, cut) if d == 0 else pl.ds(cut, chp - cut)
@@ -402,8 +403,9 @@
         p = p_ref[...].reshape(spread, ffp)
         part[g] = jnp.dot(p, hc[...], preferred_element_type=F32).reshape(NZ, NY, chp, PAIR)
 
-    def scatter_begin(g):
-        for n, d in enumerate(NEAR_ORDER):
+    def scatter_y(g, *steps):
+        for d in steps:
+            n = NEAR_ORDER.index(d)
             qy_out[g, n] = part[g, tz(d), 1 - y, :, LANES:].astype(BF16)
             start((g, "ry", d), qy_out.at[g, n], qy_in.at[g, n], other)
 
@@ -548,18 +550,27 @@
     convolve(1)
     complete(0)
     project(0)
-    scatter_begin(0)
+    scatter_y(0, 3, -3, 4)
     scatter_p(0, 0)
-    scatter_q(0, 0)
     complete(1)
     project(1)
-    scatter_begin(1)
+    scatter_y(1, 3, -3, 4)
     scatter_p(1, 0)
+    scatter_y(0, 2, -2)
+    scatter_q(0, 0)
+    scatter_y(1, 2, -2)
     scatter_q(1, 0)
-    for s in range(1, STEPS):
-        for g in range(2):
-            scatter_p(g, s)
-            scatter_q(g, s)
+    scatter_p(0, 1)
+    scatter_y(0, 1, -1)
+    scatter_q(0, 1)
+    scatter_p(1, 1)
+    scatter_y(1, 1, -1)
+    scatter_q(1, 1)
+    scatter_y(0, 0)
+    scatter_y(1, 0)
+    for g in range(2):
+        scatter_p(g, 2)
+        scatter_q(g, 2)
     scatter_pair(0)
     scatter_pair(1)
     acc = restored(0)

time: 71.8 us -> 69.2 us (0.964)
  Pallas kernels: 69.2 us -> 66.4 us
    pallas_call x1, Pallas kernels: 69.2 us -> 66.4 us  [on_device(): pl.pallas_call(functools.partial(kernel, row_devices), out_shape=jax.Shap...]
where the time goes in v6:
time: 69.2 us; the launch traced here: 68.1 us
  Pallas kernels  66.4 us (96%)
  local copies, waits for them, and re-layouts  1.67 us (2%)
    pallas_call x1, Pallas kernels, on_device(): pl.pallas_call(functools.partial(kernel, row_devices), out_shape=jax.Shap...  66.4 us
    unnamed x1, local copies, waits for them, and re-layouts  1.67 us

profile of v6, /device:TPU:16, one launch (start us, length us, event | category | flops | bytes accessed | tf_op | source)
XLA Modules:
  0.0 68.1 jit_solution(10249302006757026300)
XLA Ops:
  0.0 66.4 %shard_map.82 = bf16[4,2,64,140]{3,2,1,0:T(8,128)(2,1)} custom-call(bf16[4,2,64,140]{3,2,1,0:T(8,128)(2,1)} %x_ref.1, s32[4]{0:T(128)} %height_ref.1, s32[4]{0:T(128)} %width_ref.1, bf16[350,2,2240]{2,1,0:T(2,128)(2,1)} %bitcast.1, f32[2,350]{1,0:T(2,128)} %bias_ref.1, f32[3,3,2,350]{3,2,1,0:T(2,128)} %taps_ref.1, f32[2,350]{1,0:T(2,128)} %shift_ref.1, ...), custom_call_target="tpu_custom_call" | custom-call | tf_op jit(solution)/shard_map/pallas_call | solution.py:644
  66.4 1.7 %copy.10 = bf16[4,2,64,140]{3,2,1,0:T(8,128)(2,1)} copy(bf16[4,2,64,140]{3,2,1,0:T(8,128)(2,1)} %shard_map.82) | data formatting | bytes 286720

commit v7 on v6

--- a/solution.py
+++ b/solution.py
@@ -66,6 +66,8 @@
     xq,
     hx_out,
     hx_in,
+    hx_own,
+    hx_diag,
     ec,
     ex,
     turned,
@@ -81,6 +83,7 @@
     pf_in,
     ph_out,
     ph_in,
+    ph_diag,
     qz_out,
     qz_in,
     qy_out,
@@ -105,6 +108,7 @@
     ring = ({"tensor": y * NZ + tz(1)}, {"tensor": y * NZ + tz(-1)})
     ring2 = ({"tensor": y * NZ + tz(2)}, {"tensor": y * NZ + tz(-2)})
     other = {"tensor": (1 - y) * NZ + z}
+    diag = ({"tensor": (1 - y) * NZ + tz(1)}, {"tensor": (1 - y) * NZ + tz(-1)})
     above = {"row": (r + rows - 1) % rows}
     below = {"row": (r + 1) % rows}
 
@@ -114,7 +118,7 @@
     p_load.start()
 
     barrier = pltpu.get_barrier_semaphore()
-    for target in ring + ring2 + (other, above, below):
+    for target in ring + ring2 + diag + (other, above, below):
         pl.semaphore_signal(barrier, inc=1, device_id=target, device_id_type=MESH)
 
     pending = {}
@@ -195,28 +199,33 @@
         xq[g, y, z, 0:ch] = block[:, LANES:]
         xq[g, y, z, ch:chp] = empty
 
-    pl.semaphore_wait(barrier, 7)
+    pl.semaphore_wait(barrier, 9)
 
     def gather_begin(g):
+        for d in range(2):
+            if g == 0:
+                same((g, "own", d), xp_full.at[y, z], ring[d])
+            else:
+                start((g, "own", d), hx_out, hx_own.at[d], ring[d])
+        for d in range(2):
+            if g == 0:
+                same((g, "p", d, 0), xp_full.at[y, z], diag[d])
+            else:
+                start((g, "p", d, 0), hx_out, hx_diag.at[d], diag[d])
+        for d in range(2):
+            same((g, "q", d, 0), xq.at[g, y, z], ring[d])
+
+    def gather_own(g):
         if g == 0:
             same((g, "y"), xp_full.at[y, z], other)
-            for d in range(2):
-                same((g, "own", d), xp_full.at[y, z], ring[d])
         else:
             start((g, "y"), hx_out, hx_in, other)
-        for d in range(2):
-            same((g, "q", d, 0), xq.at[g, y, z], ring[d])
+        same((g, "qy", 0), xq.at[g, y, z], other)
 
     def gather_pair(g):
         arrived(g, "y")
-        if g == 0:
-            for d in range(2):
-                same((g, "p", d, 0), xp_full.at[1 - y, z], ring[d])
-        else:
+        if g == 1:
             xp_half[z] = hx_out[...] + hx_in[...]
-            for d in range(2):
-                same((g, "p", d, 0), xp_half.at[z], ring[d])
-        same((g, "qy", 0), xq.at[g, y, z], other)
 
     def cut_at(d):
         return pl.ds(0, cut) if d == 0 else pl.ds(cut, chp - cut)
@@ -225,8 +234,10 @@
         for d in range(2):
             zz = tz(-s if d == 0 else s)
             arrived(g, "p", d, s - 1)
-            if g == 0 and s == 1:
+            if s == 1:
                 arrived(g, "own", d)
+                if g == 1:
+                    xp_half[zz] = hx_own[d] + hx_diag[d]
             if s < STEPS:
                 src = xp_full.at[:, zz] if g == 0 else xp_half.at[zz]
                 same((g, "p", d, s), src, ring[d])
@@ -408,6 +419,8 @@
             n = NEAR_ORDER.index(d)
             qy_out[g, n] = part[g, tz(d), 1 - y, :, LANES:].astype(BF16)
             start((g, "ry", d), qy_out.at[g, n], qy_in.at[g, n], other)
+
+    last = STEPS - 1
 
     def cut_of(d):
         return slice(0, cut) if d == 0 else slice(cut, chp)
@@ -439,7 +452,12 @@
                     if s == 1 and yy == d:
                         total = total + pf_in[d, STEPS, yy].astype(F32)
                     pf_out[d, s, yy] = total.astype(BF16)
-                src, dst = pf_out.at[d, s], pf_in.at[d, s]
+                if s < last:
+                    src, dst = pf_out.at[d, s], pf_in.at[d, s]
+                else:
+                    src, dst = pf_out.at[d, s, 1 - y], pf_in.at[d, s, 1]
+                    start((g, "rpd", d), src, dst, diag[d])
+                    src, dst = pf_out.at[d, s, y], pf_in.at[d, s, 0]
             else:
                 for e in range(2):
                     at = cut_of(e)
@@ -450,6 +468,8 @@
                         total = total + ph_in[d, STEPS, at].astype(F32)
                     ph_out[d, s, at] = total.astype(BF16)
                 src, dst = ph_out.at[d, s], ph_in.at[d, s]
+                if s == last:
+                    start((g, "rpd", d), src, ph_diag.at[d], diag[d])
             start((g, "rp", d, s), src, dst, ring[d])
 
     def q_block(g, step, at):
@@ -481,22 +501,12 @@
                 src, dst = qz_out.at[g, d, STEPS, at], qz_in.at[g, d, STEPS, at]
                 start((g, "rqf", d), src, dst, ring2[d])
 
-    last = STEPS - 1
-
-    def scatter_pair(g):
-        for d in range(2):
-            arrived(g, "rp", d, last)
+    def scatter_own(g):
         if g == 0:
-            total = part[g, z, 1 - y, :, :LANES]
-            total = total + pf_in[0, last, 1 - y].astype(F32) + pf_in[1, last, 1 - y].astype(F32)
-            py_out[g] = total.astype(BF16)
+            py_out[g] = part[g, z, 1 - y, :, :LANES].astype(BF16)
         else:
-            py_out[g] = half_sum(1).astype(BF16)
+            py_out[g] = half_block(z, slice(0, chp)).astype(BF16)
         start((g, "py"), py_out.at[g], py_in.at[g], other)
-
-    def half_sum(g):
-        total = jnp.where(first, part[g, z, 0, :, :LANES], part[g, z, 1, :, :LANES])
-        return total + ph_in[0, last].astype(F32) + ph_in[1, last].astype(F32)
 
     def finish_q(g):
         for d in range(2):
@@ -507,13 +517,20 @@
         return total + qz_in[g, 0, last].astype(F32) + qz_in[g, 1, last].astype(F32)
 
     def finish_p(g):
+        arrived(g, "py")
         if g == 0:
             total = part[g, z, y, :, :LANES]
-            total = total + pf_in[0, last, y].astype(F32) + pf_in[1, last, y].astype(F32)
         else:
-            total = half_sum(1)
-        arrived(g, "py")
-        return total + py_in[g].astype(F32)
+            total = half_block(z, slice(0, chp))
+        total = total + py_in[g].astype(F32)
+        for d in range(2):
+            arrived(g, "rp", d, last)
+            arrived(g, "rpd", d)
+            if g == 0:
+                total = total + pf_in[d, last, 0].astype(F32) + pf_in[d, last, 1].astype(F32)
+            else:
+                total = total + ph_in[d, last].astype(F32) + ph_diag[d].astype(F32)
+        return total
 
     def restored(g):
         q = finish_q(g).astype(BF16)
@@ -522,12 +539,14 @@
 
     gather_begin(0)
     gather_begin(1)
+    gather_own(0)
+    gather_own(1)
     turn_columns()
-    gather_pair(0)
-    gather_pair(1)
     flatten_w()
     gather_step(0, 1)
     gather_step(1, 1)
+    gather_pair(0)
+    gather_pair(1)
     spread_w()
     gather_step(0, 2)
     gather_step(1, 2)
@@ -568,11 +587,11 @@
     scatter_q(1, 1)
     scatter_y(0, 0)
     scatter_y(1, 0)
+    scatter_own(0)
+    scatter_own(1)
     for g in range(2):
         scatter_p(g, 2)
         scatter_q(g, 2)
-    scatter_pair(0)
-    scatter_pair(1)
     acc = restored(0)
     acc = acc + restored(1)
     out_ref[...] = acc[:, :ch].astype(BF16).reshape(out_ref.shape)
@@ -616,6 +635,8 @@
         pltpu.VMEM((2, NY, NZ, chp, LANES), BF16),
         pltpu.VMEM((chp, LANES), BF16),
         pltpu.VMEM((chp, LANES), BF16),
+        pltpu.VMEM((2, chp, LANES), BF16),
+        pltpu.VMEM((2, chp, LANES), BF16),
         pltpu.VMEM((2 * ffp, PAIR), BF16),
         pltpu.VMEM((2, 2, ffp, PAIR), F32),
         pltpu.VMEM((2, 2, ffp, PAIR), F32),
@@ -631,6 +652,7 @@
         pltpu.VMEM((2, FAR, NY, chp, LANES), BF16),
         pltpu.VMEM((2, FAR, chp, LANES), BF16),
         pltpu.VMEM((2, FAR, chp, LANES), BF16),
+        pltpu.VMEM((2, chp, LANES), BF16),
         pltpu.VMEM((2, 2, FAR, chp, LANES), BF16),
         pltpu.VMEM((2, 2, FAR, chp, LANES), BF16),
         pltpu.VMEM((2, NZ, chp, LANES), BF16),

time: 69.2 us -> 65.2 us (0.942); the launches traced: 68.1 us -> 65.1 us
  Pallas kernels: 66.4 us -> 63.4 us
    pallas_call x1, Pallas kernels: 66.4 us -> 63.4 us  [on_device(): pl.pallas_call(functools.partial(kernel, row_devices), out_shape=jax.Shap...]
where the time goes in v7:
time: 65.2 us; the launch traced here: 65.1 us
  Pallas kernels  63.4 us (97%)
  local copies, waits for them, and re-layouts  1.67 us (3%)
    pallas_call x1, Pallas kernels, on_device(): pl.pallas_call(functools.partial(kernel, row_devices), out_shape=jax.Shap...  63.4 us
    unnamed x1, local copies, waits for them, and re-layouts  1.67 us

profile of v7, /device:TPU:16, one launch (start us, length us, event | category | flops | bytes accessed | tf_op | source)
XLA Modules:
  0.0 65.1 jit_solution(9175728828949284208)
XLA Ops:
  0.0 63.4 %shard_map.82 = bf16[4,2,64,140]{3,2,1,0:T(8,128)(2,1)} custom-call(bf16[4,2,64,140]{3,2,1,0:T(8,128)(2,1)} %x_ref.1, s32[4]{0:T(128)} %height_ref.1, s32[4]{0:T(128)} %width_ref.1, bf16[350,2,2240]{2,1,0:T(2,128)(2,1)} %bitcast.1, f32[2,350]{1,0:T(2,128)} %bias_ref.1, f32[3,3,2,350]{3,2,1,0:T(2,128)} %taps_ref.1, f32[2,350]{1,0:T(2,128)} %shift_ref.1, ...), custom_call_target="tpu_custom_call" | custom-call | tf_op jit(solution)/shard_map/pallas_call | solution.py:666
  63.4 1.7 %copy.10 = bf16[4,2,64,140]{3,2,1,0:T(8,128)(2,1)} copy(bf16[4,2,64,140]{3,2,1,0:T(8,128)(2,1)} %shard_map.82) | data formatting | bytes 286720

commit v8 on v7

--- a/solution.py
+++ b/solution.py
@@ -15,7 +15,7 @@
 PAIR = 2 * LANES
 BF16 = jnp.bfloat16
 F32 = jnp.float32
-NEAR_ORDER = (3, -3, 4, 2, -2, 1, -1, 0)
+NEAR_ORDER = (2, -2, 1, -1, 0)
 STEPS = FAR - 1
 
 
@@ -86,6 +86,8 @@
     ph_diag,
     qz_out,
     qz_in,
+    qd_out,
+    qd_in,
     qy_out,
     qy_in,
     py_out,
@@ -117,8 +119,9 @@
     w_load.start()
     p_load.start()
 
+    diag2 = ({"tensor": (1 - y) * NZ + tz(2)}, {"tensor": (1 - y) * NZ + tz(-2)})
     barrier = pltpu.get_barrier_semaphore()
-    for target in ring + ring2 + diag + (other, above, below):
+    for target in ring + ring2 + diag + diag2 + (other, above, below):
         pl.semaphore_signal(barrier, inc=1, device_id=target, device_id_type=MESH)
 
     pending = {}
@@ -199,7 +202,7 @@
         xq[g, y, z, 0:ch] = block[:, LANES:]
         xq[g, y, z, ch:chp] = empty
 
-    pl.semaphore_wait(barrier, 9)
+    pl.semaphore_wait(barrier, 11)
 
     def gather_begin(g):
         for d in range(2):
@@ -238,26 +241,34 @@
                 arrived(g, "own", d)
                 if g == 1:
                     xp_half[zz] = hx_own[d] + hx_diag[d]
-            if s < STEPS:
-                src = xp_full.at[:, zz] if g == 0 else xp_half.at[zz]
-                same((g, "p", d, s), src, ring[d])
+            src = xp_full.at[:, zz] if g == 0 else xp_half.at[zz]
+            same((g, "p", d, s), src, ring[d])
             if s == 2:
                 src = xp_full.at[d, zz] if g == 0 else xp_half.at[zz, cut_at(d)]
                 same((g, "pf", d), src, ring2[d])
         for d in range(2):
             zz = tz(-s if d == 0 else s)
             arrived(g, "q", d, s - 1)
-            if s < STEPS:
-                same((g, "q", d, s), xq.at[g, y, zz], ring[d])
+            same((g, "q", d, s), xq.at[g, y, zz], ring[d])
             if s == 2:
+                same((g, "qd", d), xq.at[g, y, zz], diag[d])
                 same((g, "qf", d), xq.at[g, y, zz, cut_at(d)], ring2[d])
-            same((g, "qy", -s if d == 0 else s), xq.at[g, y, zz], other)
-        if s == STEPS:
-            for d in range(2):
-                arrived(g, "qf", d)
-            same((g, "qy", FAR), xq.at[g, y, tz(FAR)], other)
-            for d in range(2):
-                arrived(g, "pf", d)
+                same((g, "qfd", d), xq.at[g, y, zz, cut_at(d)], diag2[d])
+            same((g, "qy", d, s), xq.at[g, y, zz], other)
+
+    def gathered_p(g):
+        for d in range(2):
+            arrived(g, "p", d, 2)
+            arrived(g, "pf", d)
+
+    def gathered_q(g):
+        arrived(g, "qy", 0)
+        for d in range(2):
+            arrived(g, "qy", d, 1)
+            arrived(g, "qy", d, 2)
+            for key in ("qd", "qf", "qfd"):
+                arrived(g, key, d)
+            arrived(g, "q", d, 2)
 
     def flatten_w():
         w_flat[:, wide:] = jnp.zeros((2 * ffp, w_flat.shape[1] - wide), BF16)
@@ -479,27 +490,33 @@
     def scatter_q(g, s):
         for d in range(2):
             step = STEPS - s if d == 0 else s - STEPS
-            arrived(g, "ry", step)
-            if s > 0:
+            if s == 0:
+                near = cut_of(d)
+                qz_out[g, d, 0] = part[g, tz(step), y, :, LANES:].astype(BF16)
+                qd_out[g, d, 0] = part[g, tz(step), 1 - y, :, LANES:].astype(BF16)
+                qz_out[g, d, STEPS, near] = part[g, tz(FAR), y, near, LANES:].astype(BF16)
+                qd_out[g, d, 1, near] = part[g, tz(FAR), 1 - y, near, LANES:].astype(BF16)
+                src, dst = qz_out.at[g, d, STEPS, near], qz_in.at[g, d, STEPS, near]
+                start((g, "rqf", d), src, dst, ring2[d])
+                src, dst = qd_out.at[g, d, 1, near], qd_in.at[g, d, 1, near]
+                start((g, "rqfd", d), src, dst, diag2[d])
+                start((g, "rqd", d), qd_out.at[g, d, 0], qd_in.at[g, d, 0], diag[d])
+            else:
+                arrived(g, "ry", step)
                 arrived(g, "rq", d, s - 1)
-            if s == 1:
-                arrived(g, "rqf", d)
-            for e in range(2):
-                at = cut_of(e)
-                total = q_block(g, step, at)
-                if s > 0:
-                    total = total + qz_in[g, d, s - 1, at].astype(F32)
-                if s == 1 and e == d:
-                    total = total + qz_in[g, d, STEPS, at].astype(F32)
-                qz_out[g, d, s, at] = total.astype(BF16)
+                if s == 1:
+                    for key in ("rqf", "rqfd", "rqd"):
+                        arrived(g, key, d)
+                for e in range(2):
+                    at = cut_of(e)
+                    total = q_block(g, step, at) + qz_in[g, d, s - 1, at].astype(F32)
+                    if s == 1:
+                        total = total + qd_in[g, d, 0, at].astype(F32)
+                        if e == d:
+                            total = total + qz_in[g, d, STEPS, at].astype(F32)
+                            total = total + qd_in[g, d, 1, at].astype(F32)
+                    qz_out[g, d, s, at] = total.astype(BF16)
             start((g, "rq", d, s), qz_out.at[g, d, s], qz_in.at[g, d, s], ring[d])
-        if s == 0:
-            arrived(g, "ry", FAR)
-            for d in range(2):
-                at = cut_of(d)
-                qz_out[g, d, STEPS, at] = q_block(g, FAR, at).astype(BF16)
-                src, dst = qz_out.at[g, d, STEPS, at], qz_in.at[g, d, STEPS, at]
-                start((g, "rqf", d), src, dst, ring2[d])
 
     def scatter_own(g):
         if g == 0:
@@ -553,37 +570,33 @@
     split_w()
     make_spot()
     turn_p()
-    gather_step(0, 3)
-    gather_step(1, 3)
+    gathered_p(0)
     expand_p(0)
-    for d in NEAR_ORDER:
-        arrived(0, "qy", d)
+    gathered_q(0)
     expand_q(0)
     restore(0)
+    gathered_p(1)
     expand_p(1)
-    for d in NEAR_ORDER:
-        arrived(1, "qy", d)
+    gathered_q(1)
     expand_q(1)
     restore(1)
     convolve(0)
     convolve(1)
     complete(0)
     project(0)
-    scatter_y(0, 3, -3, 4)
     scatter_p(0, 0)
+    scatter_q(0, 0)
+    scatter_y(0, 2, -2)
     complete(1)
     project(1)
-    scatter_y(1, 3, -3, 4)
     scatter_p(1, 0)
-    scatter_y(0, 2, -2)
-    scatter_q(0, 0)
+    scatter_q(1, 0)
     scatter_y(1, 2, -2)
-    scatter_q(1, 0)
+    scatter_y(0, 1, -1)
     scatter_p(0, 1)
-    scatter_y(0, 1, -1)
     scatter_q(0, 1)
+    scatter_y(1, 1, -1)
     scatter_p(1, 1)
-    scatter_y(1, 1, -1)
     scatter_q(1, 1)
     scatter_y(0, 0)
     scatter_y(1, 0)
@@ -655,6 +668,8 @@
         pltpu.VMEM((2, chp, LANES), BF16),
         pltpu.VMEM((2, 2, FAR, chp, LANES), BF16),
         pltpu.VMEM((2, 2, FAR, chp, LANES), BF16),
+        pltpu.VMEM((2, 2, 2, chp, LANES), BF16),
+        pltpu.VMEM((2, 2, 2, chp, LANES), BF16),
         pltpu.VMEM((2, NZ, chp, LANES), BF16),
         pltpu.VMEM((2, NZ, chp, LANES), BF16),
         pltpu.VMEM((2, chp, LANES), BF16),

time: 65.2 us -> 67.5 us (1.035)
  the two profiles are of different devices: /device:TPU:16 before, /device:TPU:1 now
where the time goes in v8:
time: 67.5 us; the launch traced here: 67.4 us
  Pallas kernels  65.7 us (97%)
  local copies, waits for them, and re-layouts  1.67 us (2%)
    pallas_call x1, Pallas kernels, on_device(): pl.pallas_call(functools.partial(kernel, row_devices), out_shape=jax.Shap...  65.7 us
    unnamed x1, local copies, waits for them, and re-layouts  1.67 us

profile of v8, /device:TPU:1, one launch (start us, length us, event | category | flops | bytes accessed | tf_op | source)
XLA Modules:
  0.0 67.4 jit_solution(12349888693394233981)
XLA Ops:
  0.0 65.7 %shard_map.82 = bf16[4,2,64,140]{3,2,1,0:T(8,128)(2,1)} custom-call(bf16[4,2,64,140]{3,2,1,0:T(8,128)(2,1)} %x_ref.1, s32[4]{0:T(128)} %height_ref.1, s32[4]{0:T(128)} %width_ref.1, bf16[350,2,2240]{2,1,0:T(2,128)(2,1)} %bitcast.1, f32[2,350]{1,0:T(2,128)} %bias_ref.1, f32[3,3,2,350]{3,2,1,0:T(2,128)} %taps_ref.1, f32[2,350]{1,0:T(2,128)} %shift_ref.1, ...), custom_call_target="tpu_custom_call" | custom-call | tf_op jit(solution)/shard_map/pallas_call | solution.py:681
  65.7 1.7 %copy.10 = bf16[4,2,64,140]{3,2,1,0:T(8,128)(2,1)} copy(bf16[4,2,64,140]{3,2,1,0:T(8,128)(2,1)} %shard_map.82) | data formatting | bytes 286720

commit v9 on v7

--- a/solution.py
+++ b/solution.py
@@ -162,16 +162,15 @@
     sub_row, sub_col = sub // HALF, sub % HALF
     canvas_row = row_count * r + sub_row
 
-    def make_place():
-        for g in range(2):
-            for b in range(clips):
-                limit = jnp.where(slots[b] // 2 == g, widths[b], 0)
-                first_slot = jnp.where(slots[b] == 2 * g + 1, 2 * slot_w[2 * g], 0)
-                a = first_slot + sub_row * widths[b] + sub_col
-                if g == 1:
-                    a = jnp.where(a < HALF, a + HALF * y, a + HALF)
-                ok = (sub_col < limit) & (canvas_row < heights[b])
-                place[g, b * LANES : (b + 1) * LANES] = one_hot(ok & (lane2 == a))
+    def make_place(g):
+        for b in range(clips):
+            limit = jnp.where(slots[b] // 2 == g, widths[b], 0)
+            first_slot = jnp.where(slots[b] == 2 * g + 1, 2 * slot_w[2 * g], 0)
+            a = first_slot + sub_row * widths[b] + sub_col
+            if g == 1:
+                a = jnp.where(a < HALF, a + HALF * y, a + HALF)
+            ok = (sub_col < limit) & (canvas_row < heights[b])
+            place[g, b * LANES : (b + 1) * LANES] = one_hot(ok & (lane2 == a))
 
     def make_spot():
         for g in range(2):
@@ -185,9 +184,10 @@
                     hit = (lane2 == a + HALF) | ((a < HALF) & (lane2 == a))
                 spot[g, s * LANES : (s + 1) * LANES] = one_hot(ok & hit)
 
-    make_place()
     tokens = x_ref[...].reshape(clips * LANES, ch).T
-    for g in range(2):
+
+    def make_block(g):
+        make_place(g)
         block = jnp.dot(tokens, place[g], preferred_element_type=F32).astype(BF16)
         empty = jnp.zeros((chp - ch, LANES), BF16)
         if g == 0:
@@ -199,6 +199,7 @@
         xq[g, y, z, 0:ch] = block[:, LANES:]
         xq[g, y, z, ch:chp] = empty
 
+    make_block(0)
     pl.semaphore_wait(barrier, 9)
 
     def gather_begin(g):
@@ -407,7 +408,7 @@
                 hid[at, sl] = (outs[0] * silu(outs[1])).astype(BF16)
             return 0
 
-        lax.fori_loop(0, ffp // 16, body, 0, unroll=2)
+        lax.fori_loop(0, ffp // 16, body, 0, unroll=4)
 
     def project(g):
         hc[...] = jnp.dot(hid[...], spot[g], preferred_element_type=F32).astype(BF16)
@@ -538,8 +539,9 @@
         return across(place[g, :, :LANES], p) + across(place[g, :, LANES:], q)
 
     gather_begin(0)
+    gather_own(0)
+    make_block(1)
     gather_begin(1)
-    gather_own(0)
     gather_own(1)
     turn_columns()
     flatten_w()
@@ -554,8 +556,8 @@
     make_spot()
     turn_p()
     gather_step(0, 3)
+    expand_p(0)
     gather_step(1, 3)
-    expand_p(0)
     for d in NEAR_ORDER:
         arrived(0, "qy", d)
     expand_q(0)

time: 65.2 us -> 64.2 us (0.985); the launches traced: 65.1 us -> 63.4 us
  Pallas kernels: 63.4 us -> 61.7 us
    pallas_call x1, Pallas kernels: 63.4 us -> 61.7 us  [on_device(): pl.pallas_call(functools.partial(kernel, row_devices), out_shape=jax.Shap...]
where the time goes in v9:
time: 64.2 us; the launch traced here: 63.4 us
  Pallas kernels  61.7 us (96%)
  local copies, waits for them, and re-layouts  1.67 us (3%)
    pallas_call x1, Pallas kernels, on_device(): pl.pallas_call(functools.partial(kernel, row_devices), out_shape=jax.Shap...  61.7 us
    unnamed x1, local copies, waits for them, and re-layouts  1.67 us

profile of v9, /device:TPU:16, one launch (start us, length us, event | category | flops | bytes accessed | tf_op | source)
XLA Modules:
  0.0 63.4 jit_solution(1231176449161991887)
XLA Ops:
  0.0 61.7 %shard_map.82 = bf16[4,2,64,140]{3,2,1,0:T(8,128)(2,1)} custom-call(bf16[4,2,64,140]{3,2,1,0:T(8,128)(2,1)} %x_ref.1, s32[4]{0:T(128)} %height_ref.1, s32[4]{0:T(128)} %width_ref.1, bf16[350,2,2240]{2,1,0:T(2,128)(2,1)} %bitcast.1, f32[2,350]{1,0:T(2,128)} %bias_ref.1, f32[3,3,2,350]{3,2,1,0:T(2,128)} %taps_ref.1, f32[2,350]{1,0:T(2,128)} %shift_ref.1, ...), custom_call_target="tpu_custom_call" | custom-call | tf_op jit(solution)/shard_map/pallas_call | solution.py:668
  61.7 1.7 %copy.10 = bf16[4,2,64,140]{3,2,1,0:T(8,128)(2,1)} copy(bf16[4,2,64,140]{3,2,1,0:T(8,128)(2,1)} %shard_map.82) | data formatting | bytes 286720

commit v10 on v9

--- a/solution.py
+++ b/solution.py
@@ -571,12 +571,12 @@
     convolve(1)
     complete(0)
     project(0)
+    scatter_p(0, 0)
     scatter_y(0, 3, -3, 4)
-    scatter_p(0, 0)
     complete(1)
     project(1)
+    scatter_p(1, 0)
     scatter_y(1, 3, -3, 4)
-    scatter_p(1, 0)
     scatter_y(0, 2, -2)
     scatter_q(0, 0)
     scatter_y(1, 2, -2)

time: 64.2 us -> 64.3 us (level)
  no operation moved by 1% of the time
where the time goes in v10:
time: 64.3 us; the launch traced here: 63.4 us
  Pallas kernels  61.8 us (96%)
  local copies, waits for them, and re-layouts  1.67 us (3%)
    pallas_call x1, Pallas kernels, on_device(): pl.pallas_call(functools.partial(kernel, row_devices), out_shape=jax.Shap...  61.8 us
    unnamed x1, local copies, waits for them, and re-layouts  1.67 us

profile of v10, /device:TPU:16, one launch (start us, length us, event | category | flops | bytes accessed | tf_op | source)
XLA Modules:
  0.0 63.4 jit_solution(1771581830232662484)
XLA Ops:
  0.0 61.8 %shard_map.82 = bf16[4,2,64,140]{3,2,1,0:T(8,128)(2,1)} custom-call(bf16[4,2,64,140]{3,2,1,0:T(8,128)(2,1)} %x_ref.1, s32[4]{0:T(128)} %height_ref.1, s32[4]{0:T(128)} %width_ref.1, bf16[350,2,2240]{2,1,0:T(2,128)(2,1)} %bitcast.1, f32[2,350]{1,0:T(2,128)} %bias_ref.1, f32[3,3,2,350]{3,2,1,0:T(2,128)} %taps_ref.1, f32[2,350]{1,0:T(2,128)} %shift_ref.1, ...), custom_call_target="tpu_custom_call" | custom-call | tf_op jit(solution)/shard_map/pallas_call | solution.py:668
  61.8 1.7 %copy.10 = bf16[4,2,64,140]{3,2,1,0:T(8,128)(2,1)} copy(bf16[4,2,64,140]{3,2,1,0:T(8,128)(2,1)} %shard_map.82) | data formatting | bytes 286720
